TPU v7x, 32 devices: a whole 2x2x4 slice. The times are simulated.
32 devices in a mesh: snap: 2 (over y), chan: 16 (over z, x, core).
Axes of the slice: x: 2, y: 2, z: 4, core: 2. Of those that a mesh axis runs over, the one named last changes fastest.
Arguments:
- snap_tiles: bfloat16 [16, 192, 64, 128], P('snap', 'chan'), may hold values from -6 to 6
- beam_gain: float32 [16, 64, 128], P('snap'), may hold values from 0.1 to 1
- kernel: bfloat16 [16, 32, 128, 256], P(None, 'snap'), may hold values from -0.5 to 0.5
- tile_map: int32 [16, 32], replicated, may hold values from 0 to 63
- pixel_lm: float32 [2, 8192], P(None, 'snap'), may hold values from -0.5 to 0.5
- mode_uv: int32 [2, 2048], replicated, may hold values from -32 to 31
Outputs:
- sky_cube: float32 [32, 192, 256], P('snap', 'chan')
- delay_spec: float32 [2, 192, 2048], P(None, None, ('snap', 'chan'))
Inputs may be any that keep to these rules, and one draw needn't show every extreme that they name: `tile_map`: tile indices.
All inputs are finite; a program needn't handle non-finite values.
Results may differ from a plain program's by a relative error of at most 0.0047.
Values may be sent and summed in bfloat16 or wider, within the bound.
No kernel may reach another device: no remote copies, remote signals or barrier semaphores. Data moves between devices by JAX's collectives and lax.ppermute only.
A program may use at most 192 MiB of HBM per device.

v0:
```python
import math

import jax
import jax.numpy as jnp
from jax import lax
from jax.sharding import PartitionSpec as P

BLOCK_PIX = 256


def hamming(length):
    channel_index = jnp.arange(length, dtype=jnp.float32)
    return 0.54 - 0.46 * jnp.cos(channel_index * (2.0 * math.pi / (length - 1)))


def delay_transform(power_spectrum):
    length = power_spectrum.shape[1]
    channel_index = jnp.arange(length, dtype=jnp.int32)
    residues = channel_index[:, None] * channel_index[None, :] % length
    phases = residues.astype(jnp.float32) * (2.0 * math.pi / length)
    cosine = jnp.cos(phases)
    sine_part = jnp.sin(phases)
    window_gain = hamming(length)[:, None]
    real_component = power_spectrum[0] * window_gain
    imag_part = power_spectrum[1] * window_gain
    highest = lax.Precision.HIGHEST
    out_re = jnp.dot(cosine, real_component, precision=highest) + jnp.dot(
        sine_part, imag_part, precision=highest
    )
    out_im = jnp.dot(cosine, imag_part, precision=highest) - jnp.dot(
        sine_part, real_component, precision=highest
    )
    return jnp.stack([out_re, out_im]) / math.sqrt(length)


def phasor(positions, uv_grid):
    spatial = uv_grid.astype(jnp.float32)
    phase_table = (
        positions[0][:, None] * spatial[0][None, :] + positions[1][:, None] * spatial[1][None, :]
    ) * (2.0 * math.pi)
    return jnp.concatenate([jnp.cos(phase_table), -jnp.sin(phase_table)], axis=1).astype(
        jnp.bfloat16
    )


def interpolate(weighted, kernels, block_maps):
    gathered_rows = jax.vmap(
        lambda single_snapshot_tiles, one_map: jnp.take(single_snapshot_tiles, one_map, axis=1)
    )(weighted, block_maps)
    return jnp.einsum("scbt,sbtp->bcp", gathered_rows, kernels, preferred_element_type=jnp.float32)


def per_device(snap_tiles, beam_gain, kernel, tile_map, pixel_lm, mode_uv):
    snap_count = lax.axis_size("snap")
    chan_count = lax.axis_size("chan")
    snap_index = lax.axis_index("snap")
    chan_local = snap_tiles.shape[1]
    local_pixel_blocks = pixel_lm.shape[1] // BLOCK_PIX
    block_start = snap_index * local_pixel_blocks
    weighted = (snap_tiles.astype(jnp.float32) * beam_gain[:, None]).astype(jnp.bfloat16)
    own_map = lax.dynamic_slice_in_dim(tile_map, block_start, local_pixel_blocks, 1)
    sky_cube = interpolate(lax.all_gather(weighted, "snap", axis=0, tiled=True), kernel, own_map)
    cube_low = sky_cube.astype(jnp.bfloat16)
    per_group = 2
    turn_count = local_pixel_blocks // per_group
    group_width = per_group * BLOCK_PIX
    fourier_mode_count = mode_uv.shape[1]

    def add_group(turn, running):
        partial_sky_cube = lax.dynamic_slice_in_dim(cube_low, turn * per_group, per_group, 0)
        lm_part = lax.dynamic_slice_in_dim(pixel_lm, turn * group_width, group_width, 1)
        phasor_lookup = phasor(lm_part, mode_uv).reshape(
            per_group, BLOCK_PIX, 2 * fourier_mode_count
        )
        return running + jnp.einsum(
            "woj,wjh->oh", partial_sky_cube, phasor_lookup, preferred_element_type=jnp.float32
        )

    running = lax.fori_loop(
        0, turn_count, add_group, jnp.zeros((chan_local, 2 * fourier_mode_count), jnp.float32)
    )
    partial_value = running.reshape(chan_local, 2, fourier_mode_count).transpose(1, 0, 2)
    pixel_total = pixel_lm.shape[1] * snap_count
    cell_count = fourier_mode_count // (snap_count * chan_count)
    spread = partial_value.reshape(2, chan_local, snap_count, chan_count, cell_count)
    regrouped = lax.all_to_all(spread, "chan", split_axis=3, concat_axis=1, tiled=True)
    summed = lax.psum_scatter(regrouped, "snap", scatter_dimension=2, tiled=True)
    scaled = summed.reshape(2, chan_local * chan_count, cell_count) / math.sqrt(pixel_total)
    delay_spec = delay_transform(scaled)
    return (sky_cube, delay_spec)


def solution(mesh):
    return jax.shard_map(
        per_device,
        mesh=mesh,
        in_specs=(
            P("snap", "chan", None, None),
            P("snap", None, None),
            P(None, "snap", None, None),
            P(),
            P(None, "snap"),
            P(),
        ),
        out_specs=(P("snap", "chan", None), P(None, None, ("snap", "chan"))),
        check_vma=False,
    )
```

profile of v0, /device:TPU:0, one launch (start us, length us, event | category | flops | bytes accessed | tf_op | source)
XLA Modules:
  0.0 277.3 jit_solution(12588027699825546951)
XLA Ops:
  7.2 3.1 %multiply_convert_fusion = bf16[8,12,64,128]{3,2,1,0:T(8,128)(2,1)} fusion(bf16[8,12,64,128]{3,2,1,0:T(8,128)(2,1)} %param.8, f32[8,64,128]{2,1,0:T(8,128)} %param.9), kind=kLoop, calls=%fused_computation.16 | loop fusion | flops 2359296 | bytes 3407872 | tf_op jit(solution)/shard_map/convert_element_type | solution.py:60
  10.8 47.4 %all-gather.2.cloned.1.call-done = bf16[16,12,64,128]{3,2,1,0:T(8,128)(2,1)} async-done(((bf16[8,12,64,128]{3,2,1,0:T(8,128)(2,1)}), bf16[16,12,64,128]{3,2,1,0:T(8,128)(2,1)}) %all-gather.2.cloned.1.call-update) | async-done | bytes 3145744 | tf_op jit(solution)/shard_map/all_gather | solution.py:62
  58.2 6.5 %copy.27 = bf16[16,12,64,128]{3,1,2,0:T(8,128)(2,1)} copy(bf16[16,12,64,128]{3,2,1,0:T(8,128)(2,1)} %all-gather.2.cloned.1.call-done) | data formatting | bytes 6291456 | tf_op jit(solution)/shard_map/all_gather | solution.py:62
  64.6 3.4 %gather_fusion = bf16[256,12,128]{2,1,0:T(8,128)(2,1)S(1)} fusion(bf16[16,12,64,128]{3,1,2,0:T(8,128)(2,1)} %copy.27, s32[256]{0:T(256)S(1)} %reshape.93), kind=kCustom, calls=%fused_computation | custom fusion | bytes 1574912 | tf_op jit(solution)/shard_map/vmap(jit(_take))/gather | solution.py:48
  68.1 7.0 %fusion.67 = (bf16[16,12,256]{2,1,0:T(8,128)(2,1)S(1)}, f32[16,12,256]{2,1,0:T(8,128)S(1)}) fusion(bf16[16,16,128,256]{3,2,1,0:T(8,128)(2,1)} %param.10, bf16[16,16,12,128]{3,2,1,0:T(8,128)(2,1)S(1)} %bitcast.60, pred[16,16]{0,1:T(8,128)(4,1)S(1)} %copy.26), kind=kOutput, calls=%fused_computation.74 | convolution fusion | flops 201768960 | bytes 17858816 | tf_op jit(solution)/shard_map/scbt,sbtp->bcp/dot_general | solution.py:50
  75.1 162.2 %while.16 = (s32[]{:T(128)}, f32[12,4096]{1,0:T(8,128)S(1)}, bf16[16,12,256]{2,1,0:T(8,128)(2,1)S(1)}, f32[2,4096]{1,0:T(2,128)}, f32[2,2048]{1,0:T(2,128)S(1)},...) while((s32[]{:T(128)}, f32[12,4096]{1,0:T(8,128)S(1)}, ...), condition=%wide.region_1.2_spmd.clone, body=%wide.region_0.1_spmd.clone.sunk | while | flops 66158604 | bytes 8933627 | solution.py:79
  76.0 17.1 %cosine_convert_fusion.2 = (bf16[2,256,2048]{2,1,0:T(8,128)(2,1)S(1)}, bf16[2,256,2048]{2,1,0:T(8,128)(2,1)}) fusion(f32[2048]{0:T(1024)S(1)} %bitcast.58, f32[2,256]{1,0:T(2,128)S(1)} %mul.440, f32[2048]{0:T(1024)S(1)} %bitcast.57, f32[2,256]{1,0:T(2,128)S(1)} %mul.441), kind=kLoop, calls=%fused_computation.7.clone.1 | loop fusion | flops 7340032 | bytes 4214784 | tf_op jit(solution)/shard_map/convert
  93.1 2.2 fusion.75
  96.3 17.1 %cosine_convert_fusion.2 = (bf16[2,256,2048]{2,1,0:T(8,128)(2,1)S(1)}, bf16[2,256,2048]{2,1,0:T(8,128)(2,1)}) fusion(f32[2048]{0:T(1024)S(1)} %bitcast.58, f32[2,256]{1,0:T(2,128)S(1)} %mul.440, f32[2048]{0:T(1024)S(1)} %bitcast.57, f32[2,256]{1,0:T(2,128)S(1)} %mul.441), kind=kLoop, calls=%fused_computation.7.clone.1 | loop fusion | flops 7340032 | bytes 4214784 | tf_op jit(solution)/shard_map/convert
  113.4 2.2 fusion.75
  116.5 17.1 %cosine_convert_fusion.2 = (bf16[2,256,2048]{2,1,0:T(8,128)(2,1)S(1)}, bf16[2,256,2048]{2,1,0:T(8,128)(2,1)}) fusion(f32[2048]{0:T(1024)S(1)} %bitcast.58, f32[2,256]{1,0:T(2,128)S(1)} %mul.440, f32[2048]{0:T(1024)S(1)} %bitcast.57, f32[2,256]{1,0:T(2,128)S(1)} %mul.441), kind=kLoop, calls=%fused_computation.7.clone.1 | loop fusion | flops 7340032 | bytes 4214784 | tf_op jit(solution)/shard_map/convert
  133.6 2.2 fusion.75
  136.8 17.1 %cosine_convert_fusion.2 = (bf16[2,256,2048]{2,1,0:T(8,128)(2,1)S(1)}, bf16[2,256,2048]{2,1,0:T(8,128)(2,1)}) fusion(f32[2048]{0:T(1024)S(1)} %bitcast.58, f32[2,256]{1,0:T(2,128)S(1)} %mul.440, f32[2048]{0:T(1024)S(1)} %bitcast.57, f32[2,256]{1,0:T(2,128)S(1)} %mul.441), kind=kLoop, calls=%fused_computation.7.clone.1 | loop fusion | flops 7340032 | bytes 4214784 | tf_op jit(solution)/shard_map/convert
  153.9 2.2 fusion.75
  157.1 17.1 %cosine_convert_fusion.2 = (bf16[2,256,2048]{2,1,0:T(8,128)(2,1)S(1)}, bf16[2,256,2048]{2,1,0:T(8,128)(2,1)}) fusion(f32[2048]{0:T(1024)S(1)} %bitcast.58, f32[2,256]{1,0:T(2,128)S(1)} %mul.440, f32[2048]{0:T(1024)S(1)} %bitcast.57, f32[2,256]{1,0:T(2,128)S(1)} %mul.441), kind=kLoop, calls=%fused_computation.7.clone.1 | loop fusion | flops 7340032 | bytes 4214784 | tf_op jit(solution)/shard_map/convert
  174.2 2.2 fusion.75
  177.4 17.1 %cosine_convert_fusion.2 = (bf16[2,256,2048]{2,1,0:T(8,128)(2,1)S(1)}, bf16[2,256,2048]{2,1,0:T(8,128)(2,1)}) fusion(f32[2048]{0:T(1024)S(1)} %bitcast.58, f32[2,256]{1,0:T(2,128)S(1)} %mul.440, f32[2048]{0:T(1024)S(1)} %bitcast.57, f32[2,256]{1,0:T(2,128)S(1)} %mul.441), kind=kLoop, calls=%fused_computation.7.clone.1 | loop fusion | flops 7340032 | bytes 4214784 | tf_op jit(solution)/shard_map/convert
  194.5 2.2 fusion.75
  197.6 17.1 %cosine_convert_fusion.2 = (bf16[2,256,2048]{2,1,0:T(8,128)(2,1)S(1)}, bf16[2,256,2048]{2,1,0:T(8,128)(2,1)}) fusion(f32[2048]{0:T(1024)S(1)} %bitcast.58, f32[2,256]{1,0:T(2,128)S(1)} %mul.440, f32[2048]{0:T(1024)S(1)} %bitcast.57, f32[2,256]{1,0:T(2,128)S(1)} %mul.441), kind=kLoop, calls=%fused_computation.7.clone.1 | loop fusion | flops 7340032 | bytes 4214784 | tf_op jit(solution)/shard_map/convert
  214.7 2.2 fusion.75
  217.9 17.1 %cosine_convert_fusion.2 = (bf16[2,256,2048]{2,1,0:T(8,128)(2,1)S(1)}, bf16[2,256,2048]{2,1,0:T(8,128)(2,1)}) fusion(f32[2048]{0:T(1024)S(1)} %bitcast.58, f32[2,256]{1,0:T(2,128)S(1)} %mul.440, f32[2048]{0:T(1024)S(1)} %bitcast.57, f32[2,256]{1,0:T(2,128)S(1)} %mul.441), kind=kLoop, calls=%fused_computation.7.clone.1 | loop fusion | flops 7340032 | bytes 4214784 | tf_op jit(solution)/shard_map/convert
  235.0 2.2 fusion.75
  238.3 14.4 %all_to_all.18 = f32[16,1,3072]{2,1,0:T(1,128)S(1)} all-to-all(f32[16,1,3072]{2,1,0:T(1,128)S(1)} %reshape.118), channel_id=1, replica_groups=mesh['snap'=2,'chan'=16] {'chan'}, dimensions={0} | all-to-all | bytes 393216 | tf_op jit(solution)/shard_map/all_to_all | solution.py:86
  256.5 8.1 %reduce-scatter.2.cloned.1.call-done = f32[2,192,1,1,64]{1,4,3,0,2:T(8,128)} async-done(((f32[2,192,2,1,64]{1,4,3,0,2:T(8,128)}), f32[2,192,1,1,64]{1,4,3,0,2:T(8,128)}) %reduce-scatter.2.cloned.1.call-update) | async-done | bytes 98320 | tf_op jit(solution)/shard_map/reduce_scatter | solution.py:87
  (62 shorter events, 18.4 us)
Async XLA Ops:
  7.2 3.3 %copy-start = (s32[16,32]{1,0:T(8,128)S(1)}, s32[16,32]{1,0:T(8,128)}, u32[]{:S(2)}) copy-start(s32[16,32]{1,0:T(8,128)} %param.11) | copy-start | bytes 6148
  7.2 3.6 %copy-start.1 = (s32[2,2048]{1,0:T(2,128)S(1)}, s32[2,2048]{1,0:T(2,128)}, u32[]{:S(2)}) copy-start(s32[2,2048]{1,0:T(2,128)} %param.13) | copy-start | bytes 49156
  7.2 51.0 %all-gather.2.cloned.1.call-start = ((), (), s32[]{:S(2)}) async-start(), calls=%async_computation.2 | async-start | bytes 4718592 | tf_op jit(solution)/shard_map/all_gather | solution.py:62
  10.4 254.1 %reduce-scatter.2.cloned.1.call-start = ((), (), s32[]{:S(2)}) async-start(), calls=%async_computation.3 | async-start | bytes 393216 | tf_op jit(solution)/shard_map/reduce_scatter | solution.py:87
Sparse Core Ops, SparseCore 0:
  10.5 47.6 all-gather.1
  255.7 8.7 reduce-scatter.1
where the time goes:
time: 278 us; the launch traced here: 277 us
  other arithmetic  143 us (51%)
  waiting for transfers between devices  55.4 us (20%)
  matrix products  29.4 us (11%)
  local copies, waits for them, and re-layouts  20.9 us (8%)
  blocking collectives  14.4 us (5%)
  between operations  14.1 us (5%)
    another operation x8, other arithmetic  137 us
    all_gather x1, waiting for transfers between devices, per_device(): lax.all_gather(weighted, 'snap', axis=0, tiled=True)  47.4 us
    dot_general x8, matrix products, add_group(): jnp.einsum('woj,wjh->oh', partial_sky_cube, phasor_lookup, preferred_elem...  18 us
    all_to_all x1, blocking collectives, per_device(): lax.all_to_all(spread, 'chan', split_axis=3, concat_axis=1, tiled=True)  14.4 us
    reduce_scatter x1, waiting for transfers between devices, per_device(): lax.psum_scatter(regrouped, 'snap', scatter_dimension=2, tiled=True)  8.05 us
    dot_general x1, matrix products, interpolate(): jnp.einsum('scbt,sbtp->bcp', gathered_rows, kernels, preferred_element_ty...  7.02 us
    slice x8, local copies, waits for them, and re-layouts, phasor(): positions[0][:, None] * spatial[0][None, :]  6.85 us
    all_gather x1, local copies, waits for them, and re-layouts, per_device(): lax.all_gather(weighted, 'snap', axis=0, tiled=True)  6.46 us
  transfers between devices with their start and end apart: 2, of which 2 were waited for; matrix products, arithmetic and copies ran while one was open for 0% of the time, Pallas kernels for 0%

commit v1 on v0

v1 whole, which is shorter than its diff:
```python
import math

import jax
import jax.numpy as jnp
import numpy as np
from jax import lax
from jax.experimental import pallas as pl
from jax.experimental.pallas import tpu as pltpu
from jax.sharding import PartitionSpec as P

BLOCK_PIX = 256
LANES = 128
UV_MAX = 32
TABLE_ROWS = 72


def delay_matrix(length):
    index = np.arange(length)
    window = 0.54 - 0.46 * np.cos(index * (2.0 * math.pi / (length - 1)))
    phase = (index[:, None] * index[None, :] % length) * (2.0 * math.pi / length)
    scale = window[:, None] / math.sqrt(length)
    cosine, sine = np.cos(phase) * scale, np.sin(phase) * scale
    return np.stack([np.stack([cosine, -sine], 1), np.stack([sine, cosine], 1)])


def turns(angle):
    r = (angle - jnp.round(angle)) * (2.0 * math.pi)
    return jnp.cos(r), jnp.sin(r)


def table(coord, rows):
    row = lax.broadcasted_iota(jnp.int32, (rows, coord.shape[1]), 0)
    k = jnp.where(row < UV_MAX, row, jnp.where(row < 2 * UV_MAX, row - (UV_MAX - 1), UV_MAX))
    cosine, sine = turns(k.astype(jnp.float32) * coord)
    is_sine = (row >= UV_MAX) & (row < 2 * UV_MAX)
    return jnp.where(row > 2 * UV_MAX, 0.0, jnp.where(is_sine, sine, cosine))


def gather_tiles(me, tile_map, snap_tiles, beam_gain, shifts, snap_count):
    local_snaps, chans, tiles, pix = snap_tiles.shape
    blocks = tile_map.shape[1] // snap_count
    first, count = shifts

    def body(me_ref, map_ref, tiles_ref, beam_ref, out_ref, scratch):
        s = pl.program_id(1)
        own = me_ref[0]
        dest = lax.rem(own + pl.program_id(0) + first, snap_count)
        value = tiles_ref[0].astype(jnp.float32) * beam_ref[...]
        scratch[...] = value.reshape(chans * tiles, pix)
        for b in range(blocks):
            t = map_ref[own * local_snaps + s, dest * blocks + b]
            rows = scratch[pl.ds(t, chans, stride=tiles), :]
            out_ref[0, b] = rows.astype(jnp.bfloat16)

    return pl.pallas_call(
        body,
        out_shape=jax.ShapeDtypeStruct((count, blocks, chans, local_snaps * pix), jnp.bfloat16),
        grid_spec=pltpu.PrefetchScalarGridSpec(
            num_scalar_prefetch=2,
            grid=(count, local_snaps),
            in_specs=[
                pl.BlockSpec((1, chans, tiles, pix), lambda j, s, *_: (s, 0, 0, 0)),
                pl.BlockSpec((1, tiles, pix), lambda j, s, *_: (s, 0, 0)),
            ],
            out_specs=pl.BlockSpec((1, blocks, chans, pix), lambda j, s, *_: (j, 0, 0, s)),
            scratch_shapes=[pltpu.VMEM((chans * tiles, pix), jnp.float32)],
        ),
        name="gather_tiles",
    )(me, tile_map, snap_tiles, beam_gain)


def own_part(me, own_tiles, kernel, pixel_lm):
    blocks, chans, depth = own_tiles.shape
    _, _, pix, width = kernel.shape
    local_snaps = depth // pix

    def body(me_ref, tiles_ref, kernel_ref, lm_ref, cube_ref, l_ref, m_ref):
        weights = kernel_ref[...].reshape(depth, width)
        cube_ref[0] = jnp.dot(tiles_ref[0], weights, preferred_element_type=jnp.float32)
        l_ref[...] = table(lm_ref[0:1, :], TABLE_ROWS)
        m_ref[...] = table(lm_ref[1:2, :], LANES).astype(jnp.bfloat16)

    pixels = blocks * width
    return pl.pallas_call(
        body,
        out_shape=(
            jax.ShapeDtypeStruct((blocks, chans, width), jnp.float32),
            jax.ShapeDtypeStruct((TABLE_ROWS, pixels), jnp.float32),
            jax.ShapeDtypeStruct((LANES, pixels), jnp.bfloat16),
        ),
        grid_spec=pltpu.PrefetchScalarGridSpec(
            num_scalar_prefetch=1,
            grid=(blocks,),
            in_specs=[
                pl.BlockSpec((1, chans, depth), lambda b, me: (b, 0, 0)),
                pl.BlockSpec((local_snaps, 1, pix, width), lambda b, me: (me[0], b, 0, 0)),
                pl.BlockSpec((2, width), lambda b, me: (0, b)),
            ],
            out_specs=(
                pl.BlockSpec((1, chans, width), lambda b, me: (b, 0, 0)),
                pl.BlockSpec((TABLE_ROWS, width), lambda b, me: (0, b)),
                pl.BlockSpec((LANES, width), lambda b, me: (0, b)),
            ),
        ),
        name="own_part",
    )(me, own_tiles, kernel, pixel_lm)


def uv_part(me, other_tiles, kernel, partial, l_table, m_table, mode_uv, snap_count, cells, scale):
    sources, blocks, chans, depth = other_tiles.shape
    _, _, pix, width = kernel.shape
    local_snaps = depth // pix
    modes = mode_uv.shape[1]
    owners = modes // cells
    sine_rows = slice(UV_MAX, 2 * UV_MAX)

    def select(acc, uv_ref, out_ref):
        for start in range(0, modes, LANES):
            u, v = uv_ref[0:1, start : start + LANES], uv_ref[1:2, start : start + LANES]
            sign_u = jnp.where(u < 0, -scale, scale).astype(jnp.float32)
            sign_v = jnp.where(v < 0, -1.0, 1.0).astype(jnp.float32)
            u, v = jnp.abs(u), jnp.abs(v)
            cos_lane = jnp.where(v == UV_MAX, 2 * UV_MAX, v)
            sin_lane = jnp.where(v == 0, LANES - 1, v + (UV_MAX - 1))
            cos_row = jnp.where(u == UV_MAX, 2 * UV_MAX, u)
            sin_row = jnp.where(u == 0, TABLE_ROWS - 1, u + (UV_MAX - 1))
            row = lax.broadcasted_iota(jnp.int32, (TABLE_ROWS, LANES), 0)
            is_cos = row == cos_row
            is_sin = row == sin_row
            in_sine = (row >= UV_MAX) & (row < 2 * UV_MAX)
            re_weight = jnp.where(in_sine, jnp.where(is_sin, -sign_u * sign_v, 0.0), jnp.where(is_cos, scale, 0.0))
            im_weight = jnp.where(in_sine, jnp.where(is_sin, -sign_u, 0.0), jnp.where(is_cos, -sign_v * scale, 0.0))
            cos_index = jnp.broadcast_to(cos_lane, (TABLE_ROWS, LANES))
            sin_index = jnp.broadcast_to(sin_lane, (TABLE_ROWS, LANES))
            for c in range(chans):
                grid = acc[c * TABLE_ROWS : (c + 1) * TABLE_ROWS, :]
                at_cos = jnp.take_along_axis(grid, cos_index, axis=1)
                at_sin = jnp.take_along_axis(grid, sin_index, axis=1)
                re_value = jnp.where(in_sine, at_sin, at_cos) * re_weight
                im_value = jnp.where(in_sine, at_cos, at_sin) * im_weight
                real = jnp.sum(re_value, axis=0, keepdims=True).astype(jnp.bfloat16)
                imag = jnp.sum(im_value, axis=0, keepdims=True).astype(jnp.bfloat16)
                for k in range(0, LANES, cells):
                    out_ref[(start + k) // cells, c : c + 1, :] = real[:, k : k + cells]
                    out_ref[(start + k) // cells, chans + c : chans + c + 1, :] = imag[:, k : k + cells]

    def body(me_ref, tiles_ref, kernel_ref, partial_ref, l_ref, m_ref, uv_ref, sky_ref, out_ref, cube, acc):
        b, j = pl.program_id(0), pl.program_id(1)
        weights = kernel_ref[...].reshape(depth, width)
        term = jnp.dot(tiles_ref[0, 0], weights, preferred_element_type=jnp.float32)

        @pl.when(j == 0)
        def _():
            cube[...] = partial_ref[0] + term

        @pl.when(j > 0)
        def _():
            cube[...] = cube[...] + term

        @pl.when((b == 0) & (j == 0))
        def _():
            acc[...] = jnp.zeros(acc.shape, jnp.float32)

        @pl.when(j == sources - 1)
        def _():
            sky = cube[...]
            sky_ref[:, pl.ds(b, 1), :] = sky[:, None, :]
            low = sky.astype(jnp.bfloat16).astype(jnp.float32)
            waves = l_ref[...][None] * low[:, None, :]
            waves = waves.reshape(chans * TABLE_ROWS, width).astype(jnp.bfloat16)
            acc[...] += lax.dot_general(
                waves, m_ref[...], (((1,), (1,)), ((), ())), preferred_element_type=jnp.float32
            )

        @pl.when((b == blocks - 1) & (j == sources - 1))
        def _():
            select(acc, uv_ref, out_ref)

    def source(me, j):
        return lax.rem(me[0] - j - 1 + snap_count, snap_count)

    return pl.pallas_call(
        body,
        out_shape=(
            jax.ShapeDtypeStruct((chans, blocks, width), jnp.float32),
            jax.ShapeDtypeStruct((owners, 2 * chans, cells), jnp.bfloat16),
        ),
        grid_spec=pltpu.PrefetchScalarGridSpec(
            num_scalar_prefetch=1,
            grid=(blocks, sources),
            in_specs=[
                pl.BlockSpec((1, 1, chans, depth), lambda b, j, me: (j, b, 0, 0)),
                pl.BlockSpec((local_snaps, 1, pix, width), lambda b, j, me: (source(me, j), b, 0, 0)),
                pl.BlockSpec((1, chans, width), lambda b, j, me: (b, 0, 0)),
                pl.BlockSpec((TABLE_ROWS, width), lambda b, j, me: (0, b)),
                pl.BlockSpec((LANES, width), lambda b, j, me: (0, b)),
                pl.BlockSpec((2, modes), lambda b, j, me: (0, 0)),
            ],
            out_specs=(
                pl.BlockSpec((chans, blocks, width), lambda b, j, me: (0, 0, 0)),
                pl.BlockSpec((owners, 2 * chans, cells), lambda b, j, me: (0, 0, 0)),
            ),
            scratch_shapes=[
                pltpu.VMEM((chans, width), jnp.float32),
                pltpu.VMEM((chans * TABLE_ROWS, LANES), jnp.float32),
            ],
        ),
        name="uv_part",
    )(me, other_tiles, kernel, partial, l_table, m_table, mode_uv)


def per_device(snap_tiles, beam_gain, kernel, tile_map, pixel_lm, mode_uv):
    snap_count = lax.axis_size("snap")
    chan_count = lax.axis_size("chan")
    me = lax.axis_index("snap").reshape(1).astype(jnp.int32)
    chans = snap_tiles.shape[1]
    length = chans * chan_count
    modes = mode_uv.shape[1]
    cells = modes // (snap_count * chan_count)
    pixel_total = pixel_lm.shape[1] * snap_count

    sent = gather_tiles(me, tile_map, snap_tiles, beam_gain, (1, snap_count - 1), snap_count)
    received = [
        lax.ppermute(sent[j], "snap", [(i, (i + j + 1) % snap_count) for i in range(snap_count)])[None]
        for j in range(snap_count - 1)
    ]
    own_tiles = gather_tiles(me, tile_map, snap_tiles, beam_gain, (0, 1), snap_count)[0]
    partial, l_table, m_table = own_part(me, own_tiles, kernel, pixel_lm)
    others = received[0] if len(received) == 1 else jnp.concatenate(received)
    sky, spread = uv_part(
        me, others, kernel, partial, l_table, m_table, mode_uv, snap_count, cells, 1.0 / math.sqrt(pixel_total)
    )
    regrouped = lax.all_to_all(spread, ("snap", "chan"), 0, 0, tiled=True)
    columns = regrouped.reshape(snap_count * length * 2, cells)
    matrix = delay_matrix(length).reshape(2, chan_count, chans, 2 * length).transpose(1, 0, 2, 3)
    matrix = np.concatenate([matrix.reshape(2 * length, 2 * length)] * snap_count)
    high = matrix.astype(jnp.bfloat16)
    low = (matrix - high.astype(np.float64)).astype(jnp.bfloat16)

    def transform(part):
        return lax.dot_general(
            columns, jnp.asarray(part), (((0,), (0,)), ((), ())), preferred_element_type=jnp.float32
        )

    delay = (transform(high) + transform(low)).reshape(cells, 2, length)
    return (sky.transpose(1, 0, 2), delay.transpose(1, 2, 0))


def solution(mesh):
    return jax.shard_map(
        per_device,
        mesh=mesh,
        in_specs=(
            P("snap", "chan", None, None),
            P("snap", None, None),
            P(None, "snap", None, None),
            P(),
            P(None, "snap"),
            P(),
        ),
        out_specs=(P("snap", "chan", None), P(None, None, ("snap", "chan"))),
        check_vma=False,
    )
```

time: 278 us -> 83.1 us (0.30)
  other arithmetic: 143 us -> 0 us
  Pallas kernels: 0 us -> 62.4 us
  waiting for transfers between devices: 55.4 us -> 0.01 us
  matrix products: 29.4 us -> 0.51 us
  local copies, waits for them, and re-layouts: 20.9 us -> 2.95 us
  between operations: 14.1 us -> 0.69 us
  starting transfers between devices: 0.08 us -> 2.99 us
    another operation x8 -> x0, other arithmetic: 137 us -> none
    pallas_call x0 -> x4, Pallas kernels: none -> 62.4 us  [the longest x1 34.2 us: uv_part(): pl.pallas_call(body, out_shape=(jax.ShapeDtypeStruct((chans, blocks, widt...]
    all_gather x1 -> x0, waiting for transfers between devices: 47.4 us -> none  [per_device(): lax.all_gather(weighted, 'snap', axis=0, tiled=True)]
    dot_general x13 -> x2, matrix products: 29.4 us -> 0.51 us  [transform(): lax.dot_general(columns, jnp.asarray(part), (((0,), (0,)), ((), ())), pre...]
    reduce_scatter x1 -> x0, waiting for transfers between devices: 8.05 us -> none  [per_device(): lax.psum_scatter(regrouped, 'snap', scatter_dimension=2, tiled=True)]
    slice x16 -> x0, local copies, waits for them, and re-layouts: 6.98 us -> none  [the longest x8 6.85 us: phasor(): positions[0][:, None] * spatial[0][None, :]]
    all_gather x1 -> x0, local copies, waits for them, and re-layouts: 6.46 us -> none  [per_device(): lax.all_gather(weighted, 'snap', axis=0, tiled=True)]
    gather x2 -> x0, local copies, waits for them, and re-layouts: 3.5 us -> none  [interpolate(): jnp.take(single_snapshot_tiles, one_map, axis=1)]
  transfers between devices with their start and end apart: 2 -> 1, of which waited for: 2 -> 0; matrix products, arithmetic and copies ran while one was open for 0% -> 0% of each run, Pallas kernels for 0% -> 26%
where the time goes in v1:
time: 83.1 us; the launch traced here: 82 us
  Pallas kernels  62.4 us (75%)
  blocking collectives  12.5 us (15%)
  starting transfers between devices  2.99 us (4%)
  local copies, waits for them, and re-layouts  2.95 us (4%)
    pallas_call x1, Pallas kernels, uv_part(): pl.pallas_call(body, out_shape=(jax.ShapeDtypeStruct((chans, blocks, widt...  34.2 us
    pallas_call x1, Pallas kernels, own_part(): pl.pallas_call(body, out_shape=(jax.ShapeDtypeStruct((blocks, chans, widt...  15.1 us
    pallas_call x2, Pallas kernels, gather_tiles(): pl.pallas_call(body, out_shape=jax.ShapeDtypeStruct((count, blocks, chans...  13 us
    all_to_all x1, blocking collectives, per_device(): regrouped = lax.all_to_all(spread, ('snap', 'chan'), 0, 0, tiled=True)  12.5 us
    ppermute x1, starting transfers between devices, per_device(): lax.ppermute(sent[j], 'snap', [(i, (i + j + 1) % snap_count) for i in ran...  2.99 us
    unnamed x8, local copies, waits for them, and re-layouts  2.15 us
  transfers between devices with their start and end apart: 1, of which 0 were waited for; matrix products, arithmetic and copies ran while one was open for 0% of the time, Pallas kernels for 26%

profile of v1, /device:TPU:0, one launch (start us, length us, event | category | flops | bytes accessed | tf_op | source)
XLA Modules:
  0.0 82.0 jit_solution(4749658932135446588)
XLA Ops:
  0.6 6.5 %gather_tiles.2 = bf16[1,16,12,1024]{3,2,1,0:T(8,128)(2,1)} custom-call(s32[1]{0:T(128)} %bitcast.me_ref, s32[16,32]{1,0:T(8,128)} %map_ref.3, bf16[8,12,64,128]{3,2,1,0:T(8,128)(2,1)} %tiles_ref.3, f32[8,64,128]{2,1,0:T(8,128)} %beam_ref.3), custom_call_target="tpu_custom_call" | custom-call | tf_op jit(solution)/shard_map/gather_tiles/pallas_call | solution.py:55
  7.2 3.0 %collective-permute-start = (bf16[16,12,1024]{2,1,0:T(8,128)(2,1)}, bf16[16,12,1024]{2,1,0:T(8,128)(2,1)S(1)}, u32[]{:S(2)}, u32[]{:S(2)}) collective-permute-start(bf16[16,12,1024]{2,1,0:T(8,128)(2,1)} %bitcast.17), channel_id=1, source_target_pairs={{0,16},{16,0},{1,17},{17,1},{2,18},{18,2},{3,19},{19,3},{4,20},{20... | collective-permute-start | bytes 1179656 | tf_op jit(solution)/shard_map/ppermute | solution.py:224
  10.2 6.5 %gather_tiles.3 = bf16[1,16,12,1024]{3,2,1,0:T(8,128)(2,1)} custom-call(s32[1]{0:T(128)} %bitcast.me_ref, s32[16,32]{1,0:T(8,128)} %map_ref.3, bf16[8,12,64,128]{3,2,1,0:T(8,128)(2,1)} %tiles_ref.3, f32[8,64,128]{2,1,0:T(8,128)} %beam_ref.3), custom_call_target="tpu_custom_call" | custom-call | tf_op jit(solution)/shard_map/gather_tiles/pallas_call | solution.py:55
  16.7 15.1 %own_part.1 = (f32[16,12,256]{2,1,0:T(8,128)}, f32[72,4096]{1,0:T(8,128)}, bf16[128,4096]{1,0:T(8,128)(2,1)}) custom-call(s32[1]{0:T(128)} %bitcast.me_ref, bf16[16,12,1024]{2,1,0:T(8,128)(2,1)} %bitcast.13, bf16[16,16,128,256]{3,2,1,0:T(8,128)(2,1)} %kernel_ref.3, f32[2,4096]{1,0:T(2,128)} %lm_ref.1), custom_call_target="tpu_custom_call" | custom-call | tf_op jit(solution)/shard_map/own_part/pallas_call | solution.py:84
  31.8 0.0 collective-permute-done
  31.8 0.0 copy-start.2
  31.8 0.8 copy-done.2
  32.6 0.0 copy-start
  32.6 34.2 %uv_part.1 = (f32[12,16,256]{2,1,0:T(8,128)}, bf16[32,24,64]{2,1,0:T(8,128)(2,1)}) custom-call(s32[1]{0:T(128)} %bitcast.me_ref, bf16[1,16,12,1024]{3,2,1,0:T(8,128)(2,1)} %bitcast.16, bf16[16,16,128,256]{3,2,1,0:T(8,128)(2,1)} %kernel_ref.3, f32[16,12,256]{2,1,0:T(8,128)} %get-tuple-element.7.partial_ref, f32[72,4096]{1,0:T(8,128)} %get-tuple-element.8.l_ref, ...), custom_call_target="tpu_custom_call" | custom-call | tf_op jit(solution)/shard_map/uv_part/pallas_call | solution.py:182
  66.8 0.0 copy-start.1
  66.8 1.2 %reshape.16 = bf16[32,2,768]{2,1,0:T(2,128)(2,1)S(1)} reshape(bf16[32,24,64]{2,1,0:T(8,128)(2,1)} %get-tuple-element.11) | data formatting | bytes 196608
  68.0 12.5 %all_to_all.5 = bf16[32,2,768]{2,1,0:T(2,128)(2,1)S(1)} all-to-all(bf16[32,2,768]{2,1,0:T(2,128)(2,1)S(1)} %reshape.16), channel_id=1, replica_groups=mesh['snap'=2,'chan'=16] {'snap','chan'}, dimensions={0} | all-to-all | bytes 196608 | tf_op jit(solution)/shard_map/all_to_all | solution.py:233
  80.5 0.2 reshape.17
  80.7 0.0 copy-done
  80.7 0.3 fusion
  81.0 0.0 copy-done.1
  81.0 0.3 convolution_add_fusion
  81.2 0.1 reshape.15
  81.4 0.7 copy.12
Async XLA Ops:
  7.2 24.6 %collective-permute-start = (bf16[16,12,1024]{2,1,0:T(8,128)(2,1)}, bf16[16,12,1024]{2,1,0:T(8,128)(2,1)S(1)}, u32[]{:S(2)}, u32[]{:S(2)}) collective-permute-start(bf16[16,12,1024]{2,1,0:T(8,128)(2,1)} %bitcast.17), channel_id=1, source_target_pairs={{0,16},{16,0},{1,17},{17,1},{2,18},{18,2},{3,19},{19,3},{4,20},{20... | collective-permute-start | bytes 1179656 | tf_op jit(solution)/shard_map/ppermute | solution.py:224
  31.8 0.8 copy-start.2
  32.6 48.1 %copy-start = (bf16[768,384]{1,0:T(8,128)(2,1)S(1)}, bf16[768,384]{1,0:T(8,128)(2,1)}, u32[]{:S(2)}) copy-start(bf16[768,384]{1,0:T(8,128)(2,1)} %constant.10.clone) | copy-start | bytes 1769476
  66.8 14.1 %copy-start.1 = (bf16[768,384]{1,0:T(8,128)(2,1)S(1)}, bf16[768,384]{1,0:T(8,128)(2,1)}, u32[]{:S(2)}) copy-start(bf16[768,384]{1,0:T(8,128)(2,1)} %constant.11.clone) | copy-start | bytes 1769476

commit v2 on v0

v2 whole, which is shorter than its diff:
```python
import math

import jax
import jax.numpy as jnp
import numpy as np
from jax import lax
from jax.experimental import pallas as pl
from jax.experimental.pallas import tpu as pltpu
from jax.sharding import PartitionSpec as P

LANES = 128
SUBLANES = 8
GROUP = 4
UV_MAX = 32
SINE_ROW = 40
TABLE_ROWS = SINE_ROW + UV_MAX

SMEM = pl.BlockSpec(memory_space=pltpu.SMEM)
VMEM = pl.BlockSpec(memory_space=pltpu.VMEM)
ANY = pl.BlockSpec(memory_space=pl.ANY)


def padded(chans):
    return -(-chans // SUBLANES) * SUBLANES


def delay_matrix(length):
    index = np.arange(length)
    window = 0.54 - 0.46 * np.cos(index * (2.0 * math.pi / (length - 1)))
    phase = (index[:, None] * index[None, :] % length) * (2.0 * math.pi / length)
    scale = window[:, None] / math.sqrt(length)
    cosine, sine = np.cos(phase) * scale, np.sin(phase) * scale
    return np.stack([np.stack([cosine, -sine], 1), np.stack([sine, cosine], 1)])


def cos_turns(angle):
    r = angle - jnp.round(angle)
    square = r * r
    series = jnp.float32(0.0)
    for power in (11, 9, 7, 5, 3, 1):
        term = math.pi**power / math.factorial(power) * (-1.0) ** (power // 2)
        series = series * square + term
    sine = series * r
    return 1.0 - 2.0 * sine * sine


def table(coord):
    row = lax.broadcasted_iota(jnp.int32, (TABLE_ROWS, coord.shape[1]), 0)
    is_sine = row >= SINE_ROW
    k = jnp.where(is_sine, row - (SINE_ROW - 1), row).astype(jnp.float32)
    value = cos_turns(k * coord - jnp.where(is_sine, 0.25, 0.0))
    return jnp.where((row > UV_MAX) & (row < SINE_ROW), 0.0, value)


def tile_scratch(snap_tiles, blocks):
    local_snaps, chans, tiles, pix = snap_tiles.shape
    pitch = tiles + SUBLANES
    return [
        pltpu.VMEM(snap_tiles.shape, jnp.bfloat16),
        pltpu.SemaphoreType.DMA((local_snaps,)),
        *[pltpu.VMEM((chans * pitch, pix), jnp.float32)] * 2,
        *[pltpu.VMEM((blocks * chans, pix), jnp.float32)] * 2,
    ]


def tile_copies(tiles_ref, buffer, sems):
    return [
        pltpu.make_async_copy(tiles_ref.at[s], buffer.at[s], sems.at[s]) for s in range(buffer.shape[0])
    ]


def collect(copies, own, dests, map_ref, buffer, beam_ref, spread, stage, outs):
    local_snaps, chans, tiles, pix = buffer.shape
    blocks = outs[0].shape[0] // chans
    pitch = tiles + SUBLANES
    for s in range(local_snaps):
        if copies:
            copies[s].wait()
        wide = spread[s % 2]
        for c in range(chans):
            wide[c * pitch : c * pitch + tiles, :] = buffer[s, c].astype(jnp.float32) * beam_ref[s]
        for n, (dest, out) in enumerate(zip(dests, outs)):
            rows = stage[(s + n) % 2]
            for b in range(blocks):
                t = map_ref[own * local_snaps + s, dest * blocks + b]
                rows[b * chans : (b + 1) * chans, :] = wide[pl.ds(t, chans, stride=pitch), :]
            out[:, s * pix : (s + 1) * pix] = rows[...].astype(jnp.bfloat16)


def gather_tiles(me, tile_map, snap_tiles, beam_gain, snap_count):
    local_snaps, chans, tiles, pix = snap_tiles.shape
    blocks = tile_map.shape[1] // snap_count

    def body(me_ref, map_ref, tiles_ref, beam_ref, *rest):
        outs, (buffer, sems, *work) = rest[: snap_count - 1], rest[snap_count - 1 :]
        copies = tile_copies(tiles_ref, buffer, sems)
        for copy in copies:
            copy.start()
        own = me_ref[0]
        dests = [lax.rem(own + j, snap_count) for j in range(1, snap_count)]
        collect(copies, own, dests, map_ref, buffer, beam_ref, work[:2], work[2:], outs)

    return pl.pallas_call(
        body,
        out_shape=[jax.ShapeDtypeStruct((blocks * chans, local_snaps * pix), jnp.bfloat16)] * (snap_count - 1),
        in_specs=[SMEM, SMEM, ANY, VMEM],
        out_specs=[VMEM] * (snap_count - 1),
        scratch_shapes=tile_scratch(snap_tiles, blocks),
        name="gather_tiles",
    )(me, tile_map, snap_tiles, beam_gain)


def kernel_copies(kernel_ref, slots, sems, sources, local_snaps):
    groups = kernel_ref.shape[1] // GROUP
    copies = []
    for g in range(groups):
        for source in sources:
            n = len(copies) % slots.shape[0]
            copies.append(
                pltpu.make_async_copy(
                    kernel_ref.at[pl.ds(source * local_snaps, local_snaps), pl.ds(g * GROUP, GROUP)],
                    slots.at[n],
                    sems.at[n],
                )
            )
    return copies


def kernel_scratch(kernel, local_snaps, items):
    _, _, pix, width = kernel.shape
    slots = min(items, 4)
    return [
        pltpu.VMEM((slots, local_snaps, GROUP, pix, width), jnp.bfloat16),
        pltpu.SemaphoreType.DMA((slots,)),
    ]


def group_term(tiles, slot, i, chans):
    local_snaps, _, pix, width = slot.shape
    weights = slot[:, i].reshape(local_snaps * pix, width)
    term = jnp.dot(tiles, weights, preferred_element_type=jnp.float32)
    return term[i * chans : (i + 1) * chans]


def own_part(me, tile_map, snap_tiles, beam_gain, kernel, pixel_lm, snap_count):
    local_snaps, chans, tiles, pix = snap_tiles.shape
    blocks, width = kernel.shape[1], kernel.shape[3]
    groups = blocks // GROUP
    pixels = blocks * width

    def body(me_ref, map_ref, tiles_ref, beam_ref, kernel_ref, lm_ref, cube_ref, l_ref, m_ref, *rest):
        slots, kernel_sems, gathered, buffer, sems, *work = rest
        own = me_ref[0]
        copies = tile_copies(tiles_ref, buffer, sems)
        for copy in copies:
            copy.start()
        weights = kernel_copies(kernel_ref, slots, kernel_sems, [own], local_snaps)
        for copy in weights[: slots.shape[0]]:
            copy.start()
        m_ref[TABLE_ROWS:, :] = jnp.zeros((LANES - TABLE_ROWS, pixels), jnp.bfloat16)
        for b in range(blocks):
            part = slice(b * width, (b + 1) * width)
            l_ref[:, part] = table(lm_ref[0:1, part])
            m_ref[:TABLE_ROWS, part] = table(lm_ref[1:2, part]).astype(jnp.bfloat16)
        collect(copies, own, [own], map_ref, buffer, beam_ref, work[:2], work[2:], [gathered])
        rows = GROUP * chans
        for g in range(groups):
            n = g % slots.shape[0]
            weights[g].wait()
            group_tiles = gathered[g * rows : (g + 1) * rows, :]
            for i in range(GROUP):
                start = g * rows + i * chans
                cube_ref[start : start + chans, :] = group_term(group_tiles, slots.at[n], i, chans)
            if g + slots.shape[0] < groups:
                weights[g + slots.shape[0]].start()

    return pl.pallas_call(
        body,
        out_shape=(
            jax.ShapeDtypeStruct((blocks * chans, width), jnp.float32),
            jax.ShapeDtypeStruct((TABLE_ROWS, pixels), jnp.float32),
            jax.ShapeDtypeStruct((LANES, pixels), jnp.bfloat16),
        ),
        in_specs=[SMEM, SMEM, ANY, VMEM, ANY, VMEM],
        out_specs=(VMEM, VMEM, VMEM),
        scratch_shapes=[
            *kernel_scratch(kernel, local_snaps, groups),
            pltpu.VMEM((blocks * chans, local_snaps * pix), jnp.bfloat16),
            *tile_scratch(snap_tiles, blocks),
        ],
        name="own_part",
    )(me, tile_map, snap_tiles, beam_gain, kernel, pixel_lm)


def uv_part(me, others, kernel, partial, l_table, m_table, columns, chans, cells):
    snap_count = len(others) + 1
    _, blocks, pix, width = kernel.shape
    local_snaps = others[0].shape[1] // pix
    groups = blocks // GROUP
    high = padded(chans)
    cos_rows, sin_rows = (UV_MAX + 1) * high, UV_MAX * high
    owners = columns.shape[1] // (2 * cells)
    chunk = 2 * LANES

    def select(lhs, columns_ref, out_ref):
        lane = lax.broadcasted_iota(jnp.int32, (1, chunk), 1)
        is_imag = lax.rem(lane, 2 * cells) >= cells
        row = lax.broadcasted_iota(jnp.int32, (LANES, chunk), 0)
        for start in range(0, columns.shape[1], chunk):
            u, v = columns_ref[0:1, start : start + chunk], columns_ref[1:2, start : start + chunk]
            sign_u = jnp.where(u < 0, -1.0, 1.0)
            sign_v = jnp.where(v < 0, -1.0, 1.0)
            u, v = jnp.abs(u), jnp.abs(v)
            sin_row = jnp.where(v == 0, -1, v + (SINE_ROW - 1))
            with_cos = jnp.where(row == jnp.where(is_imag, sin_row, v), jnp.where(is_imag, -sign_v, 1.0), 0.0)
            with_sin = jnp.where(
                row == jnp.where(is_imag, v, sin_row), jnp.where(is_imag, -sign_u, -sign_u * sign_v), 0.0
            )
            with_cos, with_sin = with_cos.astype(jnp.bfloat16), with_sin.astype(jnp.bfloat16)
            at_cos = jnp.dot(
                lhs[:cos_rows, :], jnp.concatenate([with_cos, with_cos]), preferred_element_type=jnp.float32
            )
            at_sin = jnp.dot(
                lhs[cos_rows:, :], jnp.concatenate([with_sin, with_sin]), preferred_element_type=jnp.float32
            )
            u = jnp.broadcast_to(u, (high, chunk))
            picked_cos = at_cos[:high]
            picked_sin = jnp.zeros((high, chunk), jnp.float32)
            for k in range(1, UV_MAX + 1):
                hit = u == k
                picked_cos = jnp.where(hit, at_cos[k * high : (k + 1) * high], picked_cos)
                picked_sin = jnp.where(hit, at_sin[(k - 1) * high : k * high], picked_sin)
            value = (picked_cos + picked_sin).astype(jnp.bfloat16)
            for k in range(0, chunk, 2 * cells):
                out_ref[(start + k) // (2 * cells)] = value[:, k : k + 2 * cells]

    def body(me_ref, *rest):
        tiles_refs, rest = rest[: len(others)], rest[len(others) :]
        kernel_ref, partial_ref, l_ref, m_ref, columns_ref, sky_ref, out_ref, slots, sems, low, acc, lhs = rest
        sources = [lax.rem(me_ref[0] + snap_count - j, snap_count) for j in range(1, snap_count)]
        weights = kernel_copies(kernel_ref, slots, sems, sources, local_snaps)
        for copy in weights[: slots.shape[0]]:
            copy.start()
        low[...] = jnp.zeros(low.shape, jnp.float32)
        rows = GROUP * chans
        for g in range(groups):
            sky = [partial_ref[g * rows + i * chans : g * rows + (i + 1) * chans, :] for i in range(GROUP)]
            for j, tiles_ref in enumerate(tiles_refs):
                item = g * len(others) + j
                weights[item].wait()
                group_tiles = tiles_ref[g * rows : (g + 1) * rows, :]
                slot = slots.at[item % slots.shape[0]]
                sky = [sky[i] + group_term(group_tiles, slot, i, chans) for i in range(GROUP)]
                if item + slots.shape[0] < len(weights):
                    weights[item + slots.shape[0]].start()
            for i in range(GROUP):
                b = g * GROUP + i
                part = slice(b * width, (b + 1) * width)
                sky_ref[:, b, :] = sky[i]
                low[i, :chans, :] = sky[i].astype(jnp.bfloat16).astype(jnp.float32)
                value = low[i][None]
                waves = jnp.concatenate(
                    [
                        (l_ref[: UV_MAX + 1, part][:, None, :] * value).reshape(cos_rows, width),
                        (l_ref[SINE_ROW:, part][:, None, :] * value).reshape(sin_rows, width),
                    ]
                ).astype(jnp.bfloat16)
                term = lax.dot_general(
                    waves, m_ref[:, part], (((1,), (1,)), ((), ())), preferred_element_type=jnp.float32
                )
                if b == 0:
                    acc[...] = term
                else:
                    acc[...] += term
        total = acc[...]
        upper = total.astype(jnp.bfloat16)
        lhs[:, :LANES] = upper
        lhs[:, LANES:] = (total - upper.astype(jnp.float32)).astype(jnp.bfloat16)
        select(lhs, columns_ref, out_ref)

    return pl.pallas_call(
        body,
        out_shape=(
            jax.ShapeDtypeStruct((chans, blocks, width), jnp.float32),
            jax.ShapeDtypeStruct((owners, high, 2 * cells), jnp.bfloat16),
        ),
        in_specs=[SMEM, *[VMEM] * len(others), ANY, VMEM, VMEM, VMEM, VMEM],
        out_specs=(VMEM, VMEM),
        scratch_shapes=[
            *kernel_scratch(kernel, local_snaps, groups * len(others)),
            pltpu.VMEM((GROUP, high, width), jnp.float32),
            pltpu.VMEM((cos_rows + sin_rows, LANES), jnp.float32),
            pltpu.VMEM((cos_rows + sin_rows, 2 * LANES), jnp.bfloat16),
        ],
        name="uv_part",
    )(me, *others, kernel, partial, l_table, m_table, columns)


def delay_part(modes, matrix, cells):
    length = matrix.shape[2] // 4

    def body(modes_ref, matrix_ref, out_ref):
        value = modes_ref[...]
        total = jnp.zeros((cells, 2 * length), jnp.float32)
        for part in range(2):
            columns = value[:, part * cells : (part + 1) * cells]
            for piece in range(2):
                total += lax.dot_general(
                    columns,
                    matrix_ref[piece, :, part * 2 * length : (part + 1) * 2 * length],
                    (((0,), (0,)), ((), ())),
                    preferred_element_type=jnp.float32,
                )
        for part in range(2):
            out_ref[part] = total[:, part * length : (part + 1) * length]

    return pl.pallas_call(
        body,
        out_shape=jax.ShapeDtypeStruct((2, cells, length), jnp.float32),
        in_specs=[VMEM, VMEM],
        out_specs=VMEM,
        name="delay_part",
    )(modes, matrix)


def per_device(snap_tiles, beam_gain, kernel, tile_map, pixel_lm, mode_uv):
    snap_count = lax.axis_size("snap")
    chan_count = lax.axis_size("chan")
    me = lax.axis_index("snap").reshape(1).astype(jnp.int32)
    chans = snap_tiles.shape[1]
    high = padded(chans)
    length = chans * chan_count
    owners = snap_count * chan_count
    cells = mode_uv.shape[1] // owners
    pixel_total = pixel_lm.shape[1] * snap_count

    sent = gather_tiles(me, tile_map, snap_tiles, beam_gain, snap_count)
    others = [
        lax.ppermute(part, "snap", [(i, (i + j) % snap_count) for i in range(snap_count)])
        for j, part in enumerate(sent, 1)
    ]
    partial, l_table, m_table = own_part(me, tile_map, snap_tiles, beam_gain, kernel, pixel_lm, snap_count)
    columns = jnp.broadcast_to(mode_uv.reshape(2, owners, 1, cells), (2, owners, 2, cells)).reshape(2, -1)
    sky, spread = uv_part(me, others, kernel, partial, l_table, m_table, columns, chans, cells)
    regrouped = lax.all_to_all(spread, ("snap", "chan"), 0, 0, tiled=True)
    matrix = delay_matrix(length) / math.sqrt(pixel_total)
    matrix = matrix.transpose(1, 0, 2, 3).reshape(chan_count, chans, 4 * length)
    matrix = np.pad(matrix, ((0, 0), (0, high - chans), (0, 0))).reshape(chan_count * high, 4 * length)
    matrix = np.concatenate([matrix] * snap_count)
    upper = matrix.astype(jnp.bfloat16)
    lower = (matrix - upper.astype(np.float64)).astype(jnp.bfloat16)
    delay = delay_part(
        regrouped.reshape(owners * high, 2 * cells), jnp.asarray(np.stack([upper, lower])), cells
    )
    return (sky.transpose(1, 0, 2), delay.transpose(0, 2, 1))


def solution(mesh):
    return jax.shard_map(
        per_device,
        mesh=mesh,
        in_specs=(
            P("snap", "chan", None, None),
            P("snap", None, None),
            P(None, "snap", None, None),
            P(),
            P(None, "snap"),
            P(),
        ),
        out_specs=(P("snap", "chan", None), P(None, None, ("snap", "chan"))),
        check_vma=False,
    )
```

time: 278 us -> 47.8 us (0.17)
  other arithmetic: 143 us -> 0 us
  waiting for transfers between devices: 55.4 us -> 1.13 us
  matrix products: 29.4 us -> 0 us
  Pallas kernels: 0 us -> 26.7 us
  local copies, waits for them, and re-layouts: 20.9 us -> 1.59 us
  between operations: 14.1 us -> 0.67 us
  starting transfers between devices: 0.08 us -> 3.06 us
    another operation x8 -> x0, other arithmetic: 137 us -> none
    all_gather x1 -> x0, waiting for transfers between devices: 47.4 us -> none  [per_device(): lax.all_gather(weighted, 'snap', axis=0, tiled=True)]
    dot_general x13 -> x0, matrix products: 29.4 us -> none  [the longest x8 18 us: add_group(): jnp.einsum('woj,wjh->oh', partial_sky_cube, phasor_lookup, preferred_elem...]
    pallas_call x0 -> x4, Pallas kernels: none -> 26.7 us  [the longest x1 13.4 us: uv_part(): pl.pallas_call(body, out_shape=(jax.ShapeDtypeStruct((chans, blocks, widt...]
    reduce_scatter x1 -> x0, waiting for transfers between devices: 8.05 us -> none  [per_device(): lax.psum_scatter(regrouped, 'snap', scatter_dimension=2, tiled=True)]
    slice x16 -> x0, local copies, waits for them, and re-layouts: 6.98 us -> none  [the longest x8 6.85 us: phasor(): positions[0][:, None] * spatial[0][None, :]]
    all_gather x1 -> x0, local copies, waits for them, and re-layouts: 6.46 us -> none  [per_device(): lax.all_gather(weighted, 'snap', axis=0, tiled=True)]
    gather x2 -> x0, local copies, waits for them, and re-layouts: 3.5 us -> none  [interpolate(): jnp.take(single_snapshot_tiles, one_map, axis=1)]
  transfers between devices with their start and end apart: 2 -> 1, of which waited for: 2 -> 1; matrix products, arithmetic and copies ran while one was open for 0% -> 2% of each run, Pallas kernels for 0% -> 15%
where the time goes in v2:
time: 47.8 us; the launch traced here: 47.5 us
  Pallas kernels  26.7 us (56%)
  blocking collectives  14.4 us (30%)
  starting transfers between devices  3.06 us (6%)
  local copies, waits for them, and re-layouts  1.59 us (3%)
  waiting for transfers between devices  1.13 us (2%)
  between operations  0.67 us (1%)
    all_to_all x1, blocking collectives, per_device(): regrouped = lax.all_to_all(spread, ('snap', 'chan'), 0, 0, tiled=True)  14.4 us
    pallas_call x1, Pallas kernels, uv_part(): pl.pallas_call(body, out_shape=(jax.ShapeDtypeStruct((chans, blocks, widt...  13.4 us
    pallas_call x1, Pallas kernels, own_part(): pl.pallas_call(body, out_shape=(jax.ShapeDtypeStruct((blocks * chans, wid...  7.34 us
    pallas_call x1, Pallas kernels, gather_tiles(): pl.pallas_call(body, out_shape=[jax.ShapeDtypeStruct((blocks * chans, loc...  3.32 us
    ppermute x1, starting transfers between devices, per_device(): lax.ppermute(part, 'snap', [(i, (i + j) % snap_count) for i in range(snap...  3.06 us
    pallas_call x1, Pallas kernels, delay_part(): pl.pallas_call(body, out_shape=jax.ShapeDtypeStruct((2, cells, length), j...  2.64 us
    ppermute x1, waiting for transfers between devices, per_device(): lax.ppermute(part, 'snap', [(i, (i + j) % snap_count) for i in range(snap...  1.13 us
  transfers between devices with their start and end apart: 1, of which 1 were waited for; matrix products, arithmetic and copies ran while one was open for 2% of the time, Pallas kernels for 15%

profile of v2, /device:TPU:0, one launch (start us, length us, event | category | flops | bytes accessed | tf_op | source)
XLA Modules:
  0.0 47.5 jit_solution(10464249557818788428)
XLA Ops:
  0.6 0.0 copy-start.1
  0.6 3.3 %gather_tiles.1 = bf16[192,1024]{1,0:T(8,128)(2,1)} custom-call(s32[1]{0:T(128)} %bitcast.me_ref, s32[16,32]{1,0:T(8,128)} %map_ref.3, bf16[8,12,64,128]{3,2,1,0:T(8,128)(2,1)} %tiles_ref.3, f32[8,64,128]{2,1,0:T(8,128)} %beam_ref.3), custom_call_target="tpu_custom_call" | custom-call | tf_op jit(solution)/shard_map/gather_tiles/pallas_call | solution.py:103
  4.0 3.1 %collective-permute-start = (bf16[192,1024]{1,0:T(8,128)(2,1)}, bf16[192,1024]{1,0:T(8,128)(2,1)S(1)}, u32[]{:S(2)}, u32[]{:S(2)}) collective-permute-start(bf16[192,1024]{1,0:T(8,128)(2,1)} %gather_tiles.1), channel_id=1, source_target_pairs={{0,16},{16,0},{1,17},{17,1},{2,18},{18,2},{3,19},{19,3},{4,20},{20... | collective-permute-start | bytes 1179656 | tf_op jit(solution)/shard_map/ppermute | solution.py:339
  7.0 0.0 copy-done.1
  7.0 0.1 broadcast_in_dim.7
  7.2 0.7 %reshape.16.rest_5_ = s32[2,4096]{1,0:T(2,128)} reshape(s32[2,32,2,64]{3,2,1,0:T(2,128)S(1)} %broadcast_in_dim.8) | data formatting | bytes 65536 | tf_op jit(solution)/shard_map/reshape | solution.py:343
  7.9 7.3 %own_part.1 = (f32[192,256]{1,0:T(8,128)}, f32[72,4096]{1,0:T(8,128)}, bf16[128,4096]{1,0:T(8,128)(2,1)}) custom-call(s32[1]{0:T(128)} %bitcast.me_ref, s32[16,32]{1,0:T(8,128)} %map_ref.3, bf16[8,12,64,128]{3,2,1,0:T(8,128)(2,1)} %tiles_ref.3, f32[8,64,128]{2,1,0:T(8,128)} %beam_ref.3, bf16[16,16,128,256]{3,2,1,0:T(8,128)(2,1)} %rest_1_.1, f32[2,4096]{1,0:T(2,128)} %lm_ref.1), custom_call_target="tpu_custom_call" | custom-call | tf_op jit(solution)/shard_map/own_part/pallas_call | solution.py:177
  15.2 1.1 %collective-permute-done.rest_0_ = bf16[192,1024]{1,0:T(8,128)(2,1)S(1)} collective-permute-done((bf16[192,1024]{1,0:T(8,128)(2,1)}, bf16[192,1024]{1,0:T(8,128)(2,1)S(1)}, u32[]{:S(2)}, u32[]{:S(2)}) %collective-permute-start) | collective-permute-done | bytes 393248 | tf_op jit(solution)/shard_map/ppermute | solution.py:339
  16.4 0.0 copy-start
  16.4 0.7 %copy-done = bf16[192,1024]{1,0:T(8,128)(2,1)} copy-done((bf16[192,1024]{1,0:T(8,128)(2,1)}, bf16[192,1024]{1,0:T(8,128)(2,1)S(1)}, u32[]{:S(2)}) %copy-start) | copy-done | bytes 393240
  17.1 13.4 %uv_part.1 = (f32[12,16,256]{2,1,0:T(8,128)}, bf16[32,16,128]{2,1,0:T(8,128)(2,1)}) custom-call(s32[1]{0:T(128)} %bitcast.me_ref, bf16[192,1024]{1,0:T(8,128)(2,1)} %copy-done, bf16[16,16,128,256]{3,2,1,0:T(8,128)(2,1)} %rest_1_.1, f32[192,256]{1,0:T(8,128)} %get-tuple-element.7.rest_2_, f32[72,4096]{1,0:T(8,128)} %get-tuple-element.8.rest_3_, ...), custom_call_target="tpu_custom_call" | custom-call | tf_op jit(solution)/shard_map/uv_part/pallas_call | solution.py:281
  30.5 14.4 %all_to_all.5 = bf16[32,16,128]{2,1,0:T(8,128)(2,1)} all-to-all(bf16[32,16,128]{2,1,0:T(8,128)(2,1)} %get-tuple-element.11), channel_id=1, replica_groups=mesh['snap'=2,'chan'=16] {'snap','chan'}, dimensions={0} | all-to-all | bytes 262144 | tf_op jit(solution)/shard_map/all_to_all | solution.py:345
  44.9 2.6 %delay_part.1 = f32[2,64,192]{2,1,0:T(8,128)} custom-call(bf16[512,128]{1,0:T(8,128)(2,1)} %bitcast.4, bf16[2,512,768]{2,1,0:T(8,128)(2,1)} %constant.8.clone.matrix_ref), custom_call_target="tpu_custom_call" | custom-call | tf_op jit(solution)/shard_map/delay_part/pallas_call | solution.py:317
  (1 shorter events, 0.0 us)
Async XLA Ops:
  0.6 6.4 %copy-start.1 = (s32[2,2048]{1,0:T(2,128)S(1)}, s32[2,2048]{1,0:T(2,128)}, u32[]{:S(2)}) copy-start(s32[2,2048]{1,0:T(2,128)} %param.12) | copy-start | bytes 49156
  4.0 12.4 %collective-permute-start = (bf16[192,1024]{1,0:T(8,128)(2,1)}, bf16[192,1024]{1,0:T(8,128)(2,1)S(1)}, u32[]{:S(2)}, u32[]{:S(2)}) collective-permute-start(bf16[192,1024]{1,0:T(8,128)(2,1)} %gather_tiles.1), channel_id=1, source_target_pairs={{0,16},{16,0},{1,17},{17,1},{2,18},{18,2},{3,19},{19,3},{4,20},{20... | collective-permute-start | bytes 1179656 | tf_op jit(solution)/shard_map/ppermute | solution.py:339
  16.4 0.7 %copy-start = (bf16[192,1024]{1,0:T(8,128)(2,1)}, bf16[192,1024]{1,0:T(8,128)(2,1)S(1)}, u32[]{:S(2)}) copy-start(bf16[192,1024]{1,0:T(8,128)(2,1)S(1)} %collective-permute-done.rest_0_) | copy-start | bytes 1179652

commit v3 on v2

v3 whole, which is shorter than its diff:
```python
import math

import jax
import jax.numpy as jnp
import numpy as np
from jax import lax
from jax.experimental import pallas as pl
from jax.experimental.pallas import tpu as pltpu
from jax.sharding import PartitionSpec as P

LANES = 128
SUBLANES = 8
GROUP = 4
PARTS = 2
UV_MAX = 32
SINE_ROW = 40
TABLE_ROWS = SINE_ROW + UV_MAX

SMEM = pl.BlockSpec(memory_space=pltpu.SMEM)
VMEM = pl.BlockSpec(memory_space=pltpu.VMEM)
HBM = pl.BlockSpec(memory_space=pltpu.HBM)


def limit(mebibytes):
    return pltpu.CompilerParams(vmem_limit_bytes=mebibytes << 20)


def padded(chans):
    return -(-chans // SUBLANES) * SUBLANES


def delay_matrix(length):
    index = np.arange(length)
    window = 0.54 - 0.46 * np.cos(index * (2.0 * math.pi / (length - 1)))
    phase = (index[:, None] * index[None, :] % length) * (2.0 * math.pi / length)
    scale = window[:, None] / math.sqrt(length)
    cosine, sine = np.cos(phase) * scale, np.sin(phase) * scale
    return np.stack([np.stack([cosine, -sine], 1), np.stack([sine, cosine], 1)])


def cos_turns(angle):
    r = angle - jnp.round(angle)
    square = r * r
    series = jnp.float32(0.0)
    for power in (11, 9, 7, 5, 3, 1):
        term = math.pi**power / math.factorial(power) * (-1.0) ** (power // 2)
        series = series * square + term
    sine = series * r
    return 1.0 - 2.0 * sine * sine


def table(coord):
    row = lax.broadcasted_iota(jnp.int32, (TABLE_ROWS, coord.shape[1]), 0)
    is_sine = row >= SINE_ROW
    k = jnp.where(is_sine, row - (SINE_ROW - 1), row).astype(jnp.float32)
    value = cos_turns(k * coord - jnp.where(is_sine, 0.25, 0.0))
    return jnp.where((row > UV_MAX) & (row < SINE_ROW), 0.0, value)


def tile_scratch(snap_tiles, blocks):
    local_snaps, chans, tiles, pix = snap_tiles.shape
    pitch = tiles + SUBLANES
    return [
        pltpu.VMEM(snap_tiles.shape, jnp.bfloat16),
        pltpu.SemaphoreType.DMA((local_snaps,)),
        *[pltpu.VMEM((chans * pitch, pix), jnp.float32)] * 2,
        *[pltpu.VMEM((blocks * chans, pix), jnp.float32)] * 2,
    ]


def tile_copies(tiles_ref, buffer, sems):
    return [
        pltpu.make_async_copy(tiles_ref.at[s], buffer.at[s], sems.at[s]) for s in range(buffer.shape[0])
    ]


def collect(copies, own, dests, map_ref, buffer, beam_ref, spread, stage, outs):
    local_snaps, chans, tiles, pix = buffer.shape
    blocks = stage[0].shape[0] // chans
    pitch = tiles + SUBLANES
    for s in range(local_snaps):
        if copies:
            copies[s].wait()
        wide = spread[s % 2]
        for c in range(chans):
            wide[c * pitch : c * pitch + tiles, :] = buffer[s, c].astype(jnp.float32) * beam_ref[s]
        for n, (dest, parts) in enumerate(zip(dests, outs)):
            rows = stage[(s + n) % 2]
            for b in range(blocks):
                t = map_ref[own * local_snaps + s, dest * blocks + b]
                rows[b * chans : (b + 1) * chans, :] = wide[pl.ds(t, chans, stride=pitch), :]
            for i, out in enumerate(parts):
                size = out.shape[0]
                out[:, s * pix : (s + 1) * pix] = rows[i * size : (i + 1) * size, :].astype(jnp.bfloat16)


def gather_tiles(tile_map, snap_tiles, beam_gain, snap_count):
    local_snaps, chans, tiles, pix = snap_tiles.shape
    blocks = tile_map.shape[1] // snap_count
    count = (snap_count - 1) * PARTS

    def body(map_ref, tiles_ref, beam_ref, *rest):
        outs, (buffer, sems, *work) = rest[:count], rest[count:]
        copies = tile_copies(tiles_ref, buffer, sems)
        for copy in copies:
            copy.start()
        own = lax.axis_index("snap")
        dests = [lax.rem(own + j, snap_count) for j in range(1, snap_count)]
        outs = [outs[n : n + PARTS] for n in range(0, count, PARTS)]
        collect(copies, own, dests, map_ref, buffer, beam_ref, work[:2], work[2:], outs)

    return pl.pallas_call(
        body,
        out_shape=[pltpu.VMEM((blocks // PARTS * chans, local_snaps * pix), jnp.bfloat16)] * count,
        in_specs=[SMEM, HBM, VMEM],
        out_specs=[VMEM] * count,
        scratch_shapes=tile_scratch(snap_tiles, blocks),
        compiler_params=limit(8),
        name="gather_tiles",
    )(tile_map, snap_tiles, beam_gain)


def kernel_copies(kernel_ref, slots, sems, sources, local_snaps, groups):
    copies = []
    for g in groups:
        for source in sources:
            n = len(copies) % slots.shape[0]
            copies.append(
                pltpu.make_async_copy(
                    kernel_ref.at[pl.ds(source * local_snaps, local_snaps), pl.ds(g * GROUP, GROUP)],
                    slots.at[n],
                    sems.at[n],
                )
            )
    return copies


def kernel_scratch(kernel, local_snaps, items):
    _, _, pix, width = kernel.shape
    slots = min(items, 4)
    return [
        pltpu.VMEM((slots, local_snaps, GROUP, pix, width), jnp.bfloat16),
        pltpu.SemaphoreType.DMA((slots,)),
    ]


def group_term(tiles, slot, i, chans):
    local_snaps, _, pix, width = slot.shape
    weights = slot[:, i].reshape(local_snaps * pix, width)
    term = jnp.dot(tiles, weights, preferred_element_type=jnp.float32)
    return term[i * chans : (i + 1) * chans]


def own_part(tile_map, snap_tiles, beam_gain, kernel, pixel_lm, columns, cells, snap_count):
    local_snaps, chans, tiles, pix = snap_tiles.shape
    blocks, width = kernel.shape[1], kernel.shape[3]
    groups = blocks // GROUP
    pixels = blocks * width

    def body(map_ref, tiles_ref, beam_ref, kernel_ref, lm_ref, columns_ref, cube_ref, l_ref, m_ref, *rest):
        ahead_ref, with_cos_ref, with_sin_ref, slots, kernel_sems, ahead_sem, gathered, buffer, sems, *work = rest
        own = lax.axis_index("snap")
        copies = tile_copies(tiles_ref, buffer, sems)
        for copy in copies:
            copy.start()
        weights = kernel_copies(kernel_ref, slots, kernel_sems, [own], local_snaps, range(groups))
        for copy in weights[: slots.shape[0]]:
            copy.start()
        m_ref[TABLE_ROWS:, :] = jnp.zeros((LANES - TABLE_ROWS, pixels), jnp.bfloat16)
        for b in range(blocks):
            part = slice(b * width, (b + 1) * width)
            l_ref[:, part] = table(lm_ref[0:1, part])
            m_ref[:TABLE_ROWS, part] = table(lm_ref[1:2, part]).astype(jnp.bfloat16)
        source = lax.rem(own + snap_count - 1, snap_count)
        ahead = pltpu.make_async_copy(
            kernel_ref.at[pl.ds(source * local_snaps, local_snaps)], ahead_ref, ahead_sem
        )
        ahead.start()
        collect(copies, own, [own], map_ref, buffer, beam_ref, work[:2], work[2:], [[gathered]])
        rows = GROUP * chans
        for g in range(groups):
            n = g % slots.shape[0]
            weights[g].wait()
            group_tiles = gathered[g * rows : (g + 1) * rows, :]
            for i in range(GROUP):
                start = g * rows + i * chans
                cube_ref[start : start + chans, :] = group_term(group_tiles, slots.at[n], i, chans)
            if g + slots.shape[0] < groups:
                weights[g + slots.shape[0]].start()
        pick_v(columns_ref, with_cos_ref, with_sin_ref, cells)
        ahead.wait()

    return pl.pallas_call(
        body,
        out_shape=(
            pltpu.VMEM((blocks * chans, width), jnp.float32),
            pltpu.VMEM((TABLE_ROWS, pixels), jnp.float32),
            pltpu.VMEM((LANES, pixels), jnp.bfloat16),
            pltpu.VMEM((local_snaps, blocks, pix, width), jnp.bfloat16),
            pltpu.VMEM((LANES, columns.shape[1]), jnp.bfloat16),
            pltpu.VMEM((LANES, columns.shape[1]), jnp.bfloat16),
        ),
        in_specs=[SMEM, HBM, VMEM, HBM, VMEM, VMEM],
        out_specs=(VMEM,) * 6,
        scratch_shapes=[
            *kernel_scratch(kernel, local_snaps, groups),
            pltpu.SemaphoreType.DMA,
            pltpu.VMEM((blocks * chans, local_snaps * pix), jnp.bfloat16),
            *tile_scratch(snap_tiles, blocks),
        ],
        compiler_params=limit(24),
        name="own_part",
    )(tile_map, snap_tiles, beam_gain, kernel, pixel_lm, columns)


def pick_v(columns_ref, with_cos_ref, with_sin_ref, cells):
    chunk = 2 * LANES
    lane = lax.broadcasted_iota(jnp.int32, (1, chunk), 1)
    row = lax.broadcasted_iota(jnp.int32, (LANES, chunk), 0)
    for start in range(0, columns_ref.shape[1], chunk):
        part = slice(start, start + chunk)
        is_imag = lax.rem(lane, 2 * cells) >= cells
        u, v = columns_ref[0:1, part], columns_ref[1:2, part]
        sign_u = jnp.where(u < 0, -1.0, 1.0)
        sign_v = jnp.where(v < 0, -1.0, 1.0)
        v = jnp.abs(v)
        sin_row = jnp.where(v == 0, -1, v + (SINE_ROW - 1))
        with_cos = jnp.where(row == jnp.where(is_imag, sin_row, v), jnp.where(is_imag, -sign_v, 1.0), 0.0)
        with_sin = jnp.where(
            row == jnp.where(is_imag, v, sin_row), jnp.where(is_imag, -sign_u, -sign_u * sign_v), 0.0
        )
        with_cos_ref[:, part] = with_cos.astype(jnp.bfloat16)
        with_sin_ref[:, part] = with_sin.astype(jnp.bfloat16)


def uv_part(others, kernel, ahead, partial, l_table, m_table, first_group, chans, begun=None, picks=None, cells=0):
    snap_count = len(others) + 1
    _, blocks, pix, width = kernel.shape
    local_snaps = others[0].shape[1] // pix
    rows = GROUP * chans
    groups = range(first_group, first_group + others[0].shape[0] // rows)
    high = padded(chans)
    cos_rows, sin_rows = (UV_MAX + 1) * high, UV_MAX * high
    later = len(others) - 1
    last = begun is not None

    def select(lhs, columns_ref, with_cos_ref, with_sin_ref, out_ref):
        chunk = 2 * LANES
        for start in range(0, columns_ref.shape[1], chunk):
            part = slice(start, start + chunk)
            with_cos, with_sin = with_cos_ref[:, part], with_sin_ref[:, part]
            at_cos = jnp.dot(
                lhs[:cos_rows, :], jnp.concatenate([with_cos, with_cos]), preferred_element_type=jnp.float32
            )
            at_sin = jnp.dot(
                lhs[cos_rows:, :], jnp.concatenate([with_sin, with_sin]), preferred_element_type=jnp.float32
            )
            u = jnp.broadcast_to(jnp.abs(columns_ref[0:1, part]), (high, chunk))
            picked_cos = at_cos[:high]
            picked_sin = jnp.zeros((high, chunk), jnp.float32)
            for k in range(1, UV_MAX + 1):
                hit = u == k
                picked_cos = jnp.where(hit, at_cos[k * high : (k + 1) * high], picked_cos)
                picked_sin = jnp.where(hit, at_sin[(k - 1) * high : k * high], picked_sin)
            value = (picked_cos + picked_sin).astype(jnp.bfloat16)
            for k in range(0, chunk, 2 * cells):
                out_ref[(start + k) // (2 * cells)] = value[:, k : k + 2 * cells]

    def body(*rest):
        tiles_refs, rest = rest[: len(others)], rest[len(others) :]
        kernel_ref, ahead_ref, partial_ref, l_ref, m_ref, *rest = rest
        if last:
            begun_cube, begun_acc, columns_ref, with_cos_ref, with_sin_ref, sky_ref, out_ref, low, acc, lhs, *rest = rest
        else:
            cube_ref, acc, low, *rest = rest
        if later:
            slots, sems = rest
            own = lax.axis_index("snap")
            sources = [lax.rem(own + snap_count - j, snap_count) for j in range(2, snap_count)]
            weights = kernel_copies(kernel_ref, slots, sems, sources, local_snaps, groups)
            for copy in weights[: slots.shape[0]]:
                copy.start()
        low[...] = jnp.zeros(low.shape, jnp.float32)
        if last:
            for b in range(first_group * GROUP):
                sky_ref[:, b, :] = begun_cube[b * chans : (b + 1) * chans, :]
        for n, g in enumerate(groups):
            sky = [partial_ref[g * rows + i * chans : g * rows + (i + 1) * chans, :] for i in range(GROUP)]
            near = ahead_ref.at[:, g * GROUP : (g + 1) * GROUP]
            group_tiles = tiles_refs[0][n * rows : (n + 1) * rows, :]
            sky = [sky[i] + group_term(group_tiles, near, i, chans) for i in range(GROUP)]
            for j in range(later):
                item = n * later + j
                weights[item].wait()
                group_tiles = tiles_refs[j + 1][n * rows : (n + 1) * rows, :]
                slot = slots.at[item % slots.shape[0]]
                sky = [sky[i] + group_term(group_tiles, slot, i, chans) for i in range(GROUP)]
                if item + slots.shape[0] < len(weights):
                    weights[item + slots.shape[0]].start()
            for i in range(GROUP):
                b = g * GROUP + i
                part = slice(b * width, (b + 1) * width)
                if last:
                    sky_ref[:, b, :] = sky[i]
                else:
                    cube_ref[b * chans : (b + 1) * chans, :] = sky[i]
                low[i, :chans, :] = sky[i].astype(jnp.bfloat16).astype(jnp.float32)
                value = low[i][None]
                waves = jnp.concatenate(
                    [
                        (l_ref[: UV_MAX + 1, part][:, None, :] * value).reshape(cos_rows, width),
                        (l_ref[SINE_ROW:, part][:, None, :] * value).reshape(sin_rows, width),
                    ]
                ).astype(jnp.bfloat16)
                term = lax.dot_general(
                    waves, m_ref[:, part], (((1,), (1,)), ((), ())), preferred_element_type=jnp.float32
                )
                if n or i:
                    acc[...] += term
                elif last:
                    acc[...] = begun_acc[...] + term
                else:
                    acc[...] = term
        if last:
            total = acc[...]
            upper = total.astype(jnp.bfloat16)
            lhs[:, :LANES] = upper
            lhs[:, LANES:] = (total - upper.astype(jnp.float32)).astype(jnp.bfloat16)
            select(lhs, columns_ref, with_cos_ref, with_sin_ref, out_ref)

    grid_shape = (cos_rows + sin_rows, LANES)
    scratch = [pltpu.VMEM((GROUP, high, width), jnp.float32)]
    operands = [*others, kernel, ahead, partial, l_table, m_table]
    if last:
        columns, with_cos, with_sin = picks
        operands += [*begun, columns, with_cos, with_sin]
        out_shape = (
            pltpu.VMEM((chans, blocks, width), jnp.float32),
            pltpu.VMEM((columns.shape[1] // (2 * cells), high, 2 * cells), jnp.bfloat16),
        )
        scratch += [pltpu.VMEM(grid_shape, jnp.float32), pltpu.VMEM((cos_rows + sin_rows, 2 * LANES), jnp.bfloat16)]
    else:
        out_shape = (
            pltpu.VMEM((groups.stop * rows, width), jnp.float32),
            pltpu.VMEM(grid_shape, jnp.float32),
        )
    if later:
        scratch += kernel_scratch(kernel, local_snaps, len(groups) * later)
    return pl.pallas_call(
        body,
        out_shape=out_shape,
        in_specs=[HBM if operand is kernel else VMEM for operand in operands],
        out_specs=(VMEM, VMEM),
        scratch_shapes=scratch,
        compiler_params=limit(24 if later else 12),
        name="uv_last" if last else "uv_first",
    )(*operands)


def delay_part(modes, matrix, cells):
    length = matrix.shape[2] // 4

    def body(modes_ref, matrix_ref, out_ref):
        value = modes_ref[...]
        total = jnp.zeros((cells, 2 * length), jnp.float32)
        for part in range(2):
            columns = value[:, part * cells : (part + 1) * cells]
            for piece in range(2):
                total += lax.dot_general(
                    columns,
                    matrix_ref[piece, :, part * 2 * length : (part + 1) * 2 * length],
                    (((0,), (0,)), ((), ())),
                    preferred_element_type=jnp.float32,
                )
        for part in range(2):
            out_ref[part] = total[:, part * length : (part + 1) * length]

    return pl.pallas_call(
        body,
        out_shape=jax.ShapeDtypeStruct((2, cells, length), jnp.float32),
        in_specs=[VMEM, VMEM],
        out_specs=VMEM,
        compiler_params=limit(8),
        name="delay_part",
    )(modes, matrix)


def per_device(snap_tiles, beam_gain, kernel, tile_map, pixel_lm, mode_uv):
    snap_count = lax.axis_size("snap")
    chan_count = lax.axis_size("chan")
    chans = snap_tiles.shape[1]
    high = padded(chans)
    length = chans * chan_count
    owners = snap_count * chan_count
    cells = mode_uv.shape[1] // owners
    pixel_total = pixel_lm.shape[1] * snap_count

    snap_tiles, kernel, tile_map = (
        pltpu.with_memory_space_constraint(value, pltpu.HBM) for value in (snap_tiles, kernel, tile_map)
    )
    sent = gather_tiles(tile_map, snap_tiles, pltpu.with_memory_space_constraint(beam_gain, pltpu.HBM), snap_count)
    others = [
        lax.ppermute(part, "snap", [(i, (i + n // PARTS + 1) % snap_count) for i in range(snap_count)])
        for n, part in enumerate(sent)
    ]
    columns = jnp.broadcast_to(mode_uv.reshape(2, owners, 1, cells), (2, owners, 2, cells)).reshape(2, -1)
    partial, l_table, m_table, ahead, *picks = own_part(
        tile_map, snap_tiles, beam_gain, kernel, pixel_lm, columns, cells, snap_count
    )
    shared = (kernel, ahead, partial, l_table, m_table)
    begun = uv_part(others[0::PARTS], *shared, 0, chans)
    half = kernel.shape[1] // GROUP // PARTS
    sky, spread = uv_part(others[1::PARTS], *shared, half, chans, begun, (columns, *picks), cells)
    regrouped = lax.all_to_all(spread, ("snap", "chan"), 0, 0, tiled=True)
    matrix = delay_matrix(length) / math.sqrt(pixel_total)
    matrix = matrix.transpose(1, 0, 2, 3).reshape(chan_count, chans, 4 * length)
    matrix = np.pad(matrix, ((0, 0), (0, high - chans), (0, 0))).reshape(chan_count * high, 4 * length)
    matrix = np.concatenate([matrix] * snap_count)
    upper = matrix.astype(jnp.bfloat16)
    lower = (matrix - upper.astype(np.float64)).astype(jnp.bfloat16)
    delay = delay_part(
        regrouped.reshape(owners * high, 2 * cells), jnp.asarray(np.stack([upper, lower])), cells
    )
    return (sky.transpose(1, 0, 2), delay.transpose(0, 2, 1))


def solution(mesh):
    return jax.shard_map(
        per_device,
        mesh=mesh,
        in_specs=(
            P("snap", "chan", None, None),
            P("snap", None, None),
            P(None, "snap", None, None),
            P(),
            P(None, "snap"),
            P(),
        ),
        out_specs=(P("snap", "chan", None), P(None, None, ("snap", "chan"))),
        check_vma=False,
    )
```

time: 47.8 us -> 39 us (0.82)
  blocking collectives: 14.4 us -> 0 us
  Pallas kernels: 26.7 us -> 20.1 us
  waiting for transfers between devices: 1.13 us -> 7.53 us
  starting transfers between devices: 3.06 us -> 9.44 us
  local copies, waits for them, and re-layouts: 1.59 us -> 0.93 us
    all_to_all x1 -> x0, blocking collectives: 14.4 us -> none  [per_device(): regrouped = lax.all_to_all(spread, ('snap', 'chan'), 0, 0, tiled=True)]
    all_to_all x0 -> x1, waiting for transfers between devices: none -> 7.52 us  [per_device(): regrouped = lax.all_to_all(spread, ('snap', 'chan'), 0, 0, tiled=True)]
    all_to_all x0 -> x1, starting transfers between devices: none -> 6.3 us  [per_device(): regrouped = lax.all_to_all(spread, ('snap', 'chan'), 0, 0, tiled=True)]
    pallas_call x3 -> x4, Pallas kernels: 24 us -> 19 us  [the longest x2 9.01 us: uv_part(): pl.pallas_call(body, out_shape=out_shape, in_specs=[HBM if operand is ker...]
    pallas_call x1, Pallas kernels: 2.64 us -> 1.15 us  [delay_part(): pl.pallas_call(body, out_shape=jax.ShapeDtypeStruct((2, cells, length), j...]
    ppermute x1 -> x2, waiting for transfers between devices: 1.13 us -> 0.01 us  [per_device(): lax.ppermute(part, 'snap', [(i, (i + n // PARTS + 1) % snap_count) for i...]
    reshape x1, local copies, waits for them, and re-layouts: 0.73 us -> 0.12 us  [per_device(): jnp.broadcast_to(mode_uv.reshape(2, owners, 1, cells), (2, owners, 2, cel...]
    ppermute x1 -> x2, starting transfers between devices: 3.06 us -> 3.14 us  [per_device(): lax.ppermute(part, 'snap', [(i, (i + n // PARTS + 1) % snap_count) for i...]
  transfers between devices with their start and end apart: 1 -> 3, of which waited for: 1 -> 1; matrix products, arithmetic and copies ran while one was open for 2% -> 2% of each run, Pallas kernels for 15% -> 26%
where the time goes in v3:
time: 39 us; the launch traced here: 38.8 us
  Pallas kernels  20.1 us (52%)
  starting transfers between devices  9.44 us (24%)
  waiting for transfers between devices  7.53 us (19%)
  local copies, waits for them, and re-layouts  0.93 us (2%)
  between operations  0.73 us (2%)
    pallas_call x2, Pallas kernels, uv_part(): pl.pallas_call(body, out_shape=out_shape, in_specs=[HBM if operand is ker...  9.01 us
    all_to_all x1, waiting for transfers between devices, per_device(): regrouped = lax.all_to_all(spread, ('snap', 'chan'), 0, 0, tiled=True)  7.52 us
    pallas_call x1, Pallas kernels, own_part(): pl.pallas_call(body, out_shape=(pltpu.VMEM((blocks * chans, width), jnp.f...  7.35 us
    all_to_all x1, starting transfers between devices, per_device(): regrouped = lax.all_to_all(spread, ('snap', 'chan'), 0, 0, tiled=True)  6.3 us
    ppermute x2, starting transfers between devices, per_device(): lax.ppermute(part, 'snap', [(i, (i + n // PARTS + 1) % snap_count) for i...  3.14 us
    pallas_call x1, Pallas kernels, gather_tiles(): pl.pallas_call(body, out_shape=[pltpu.VMEM((blocks // PARTS * chans, loca...  2.62 us
    pallas_call x1, Pallas kernels, delay_part(): pl.pallas_call(body, out_shape=jax.ShapeDtypeStruct((2, cells, length), j...  1.15 us
  transfers between devices with their start and end apart: 3, of which 1 were waited for; matrix products, arithmetic and copies ran while one was open for 2% of the time, Pallas kernels for 26%

profile of v3, /device:TPU:0, one launch (start us, length us, event | category | flops | bytes accessed | tf_op | source)
XLA Modules:
  0.0 38.8 jit_solution(17461885883806737625)
XLA Ops:
  0.6 0.0 copy-start.1
  0.6 0.0 copy-start.3
  0.7 0.0 copy-start.2
  0.7 2.6 %gather_tiles.1 = (bf16[96,1024]{1,0:T(8,128)(2,1)S(1)}, bf16[96,1024]{1,0:T(8,128)(2,1)S(1)}) custom-call(s32[16,32]{1,0:T(8,128)} %map_ref.3, bf16[8,12,64,128]{3,2,1,0:T(8,128)(2,1)} %tiles_ref.3, f32[8,64,128]{2,1,0:T(8,128)} %beam_ref.3), custom_call_target="tpu_custom_call" | custom-call | tf_op jit(solution)/shard_map/gather_tiles/pallas_call | solution.py:112
  3.3 3.1 %collective-permute-start.1 = (bf16[96,1024]{1,0:T(8,128)(2,1)S(1)}, bf16[96,1024]{1,0:T(8,128)(2,1)S(1)}, u32[]{:S(2)}, u32[]{:S(2)}) collective-permute-start(bf16[96,1024]{1,0:T(8,128)(2,1)S(1)} %get-tuple-element.19), channel_id=1, source_target_pairs={{0,16},{16,0},{1,17},{17,1},{2,18},{18,2},{3,19},{19,3},{4,20},{20... | collective-permute-start | bytes 589832 | tf_op jit(solution)/shard_map/ppermute | solution.py:403
  6.4 0.1 collective-permute-start
  6.4 0.0 copy-done.3
  6.4 0.1 broadcast_in_dim.7
  6.6 0.1 reshape.12.columns_ref.rest_8_
  6.7 0.0 copy-done.1
  6.7 0.0 copy-done.2
  6.7 7.4 %own_part.1 = (f32[192,256]{1,0:T(8,128)S(1)}, f32[72,4096]{1,0:T(8,128)S(1)}, bf16[128,4096]{1,0:T(8,128)(2,1)S(1)}, bf16[8,16,128,256]{3,2,1,0:T(8,128)(2,1)S(...) custom-call(s32[16,32]{1,0:T(8,128)} %map_ref.3, bf16[8,12,64,128]{3,2,1,0:T(8,128)(2,1)} %tiles_ref.3, ...), custom_call_target="tpu_custom_call" | custom-call | tf_op jit(solution)/shard_map/own_part/pallas_call | solution.py:193
  14.1 0.0 collective-permute-done.1.rest_0_
  14.1 2.7 %uv_first.1 = (f32[96,256]{1,0:T(8,128)S(1)}, f32[1040,128]{1,0:T(8,128)S(1)}) custom-call(bf16[96,1024]{1,0:T(8,128)(2,1)S(1)} %collective-permute-done.1.rest_0_, bf16[16,16,128,256]{3,2,1,0:T(8,128)(2,1)} %rest_1_.3, bf16[8,16,128,256]{3,2,1,0:T(8,128)(2,1)S(1)} %get-tuple-element.15.rest_2_, f32[192,256]{1,0:T(8,128)S(1)} %get-tuple-element.16.rest_3_, ...), custom_call_target="tpu_custom_call" | custom-call | tf_op jit(solution)/shard_map/uv_first/pallas_call | solution.py:349
  16.8 0.0 collective-permute-done.rest_0_
  16.8 0.0 copy-start
  16.8 6.3 %uv_last.1 = (f32[12,16,256]{2,1,0:T(8,128)S(1)}, bf16[32,16,128]{2,1,0:T(8,128)(2,1)}) custom-call(bf16[96,1024]{1,0:T(8,128)(2,1)S(1)} %collective-permute-done.rest_0_, bf16[16,16,128,256]{3,2,1,0:T(8,128)(2,1)} %rest_1_.3, bf16[8,16,128,256]{3,2,1,0:T(8,128)(2,1)S(1)} %get-tuple-element.15.rest_2_, f32[192,256]{1,0:T(8,128)S(1)} %get-tuple-element.16.rest_3_, ...), custom_call_target="tpu_custom_call" | custom-call | tf_op jit(solution)/shard_map/uv_last/pallas_call | solution.py:349
  23.1 6.3 %all-to-all-start = ((bf16[32,16,128]{2,1,0:T(8,128)(2,1)}), bf16[32,16,128]{2,1,0:T(8,128)(2,1)S(1)}, u32[]{:S(2)}, u32[]{:S(2)}) async-start(bf16[32,16,128]{2,1,0:T(8,128)(2,1)} %get-tuple-element.25), calls=%async_computation | async-start | bytes 262144 | tf_op jit(solution)/shard_map/all_to_all | solution.py:414
  29.4 0.7 %copy.9 = f32[16,12,256]{2,0,1:T(8,128)} copy(f32[16,12,256]{2,0,1:T(8,128)S(1)} %bitcast.3) | data formatting | bytes 393216
  30.1 7.5 %all-to-all-done = bf16[32,16,128]{2,1,0:T(8,128)(2,1)S(1)} async-done(((bf16[32,16,128]{2,1,0:T(8,128)(2,1)}), bf16[32,16,128]{2,1,0:T(8,128)(2,1)S(1)}, u32[]{:S(2)}, u32[]{:S(2)}) %all-to-all-start) | async-done | bytes 131104 | tf_op jit(solution)/shard_map/all_to_all | solution.py:414
  37.6 0.0 copy-done
  37.6 1.2 %delay_part.1 = f32[2,64,192]{2,1,0:T(8,128)} custom-call(bf16[512,128]{1,0:T(8,128)(2,1)S(1)} %bitcast.4, bf16[2,512,768]{2,1,0:T(8,128)(2,1)S(1)} %copy-done), custom_call_target="tpu_custom_call" | custom-call | tf_op jit(solution)/shard_map/delay_part/pallas_call | solution.py:378
  (1 shorter events, 0.0 us)
Async XLA Ops:
  0.6 6.0 %copy-start.1 = (f32[8,64,128]{2,1,0:T(8,128)S(1)}, f32[8,64,128]{2,1,0:T(8,128)}, u32[]{:S(2)}) copy-start(f32[8,64,128]{2,1,0:T(8,128)} %beam_ref.3) | copy-start | bytes 786436
  0.6 5.8 %copy-start.3 = (s32[2,2048]{1,0:T(2,128)S(1)}, s32[2,2048]{1,0:T(2,128)}, u32[]{:S(2)}) copy-start(s32[2,2048]{1,0:T(2,128)} %param.12) | copy-start | bytes 49156
  0.7 6.0 %copy-start.2 = (f32[2,4096]{1,0:T(2,128)S(1)}, f32[2,4096]{1,0:T(2,128)}, u32[]{:S(2)}) copy-start(f32[2,4096]{1,0:T(2,128)} %lm_ref.1) | copy-start | bytes 98308
  3.3 10.8 %collective-permute-start.1 = (bf16[96,1024]{1,0:T(8,128)(2,1)S(1)}, bf16[96,1024]{1,0:T(8,128)(2,1)S(1)}, u32[]{:S(2)}, u32[]{:S(2)}) collective-permute-start(bf16[96,1024]{1,0:T(8,128)(2,1)S(1)} %get-tuple-element.19), channel_id=1, source_target_pairs={{0,16},{16,0},{1,17},{17,1},{2,18},{18,2},{3,19},{19,3},{4,20},{20... | collective-permute-start | bytes 589832 | tf_op jit(solution)/shard_map/ppermute | solution.py:403
  6.4 10.4 %collective-permute-start = (bf16[96,1024]{1,0:T(8,128)(2,1)S(1)}, bf16[96,1024]{1,0:T(8,128)(2,1)S(1)}, u32[]{:S(2)}, u32[]{:S(2)}) collective-permute-start(bf16[96,1024]{1,0:T(8,128)(2,1)S(1)} %get-tuple-element.14), channel_id=1, source_target_pairs={{0,16},{16,0},{1,17},{17,1},{2,18},{18,2},{3,19},{19,3},{4,20},{20... | collective-permute-start | bytes 589832 | tf_op jit(solution)/shard_map/ppermute | solution.py:403
  16.8 20.8 %copy-start = (bf16[2,512,768]{2,1,0:T(8,128)(2,1)S(1)}, bf16[2,512,768]{2,1,0:T(8,128)(2,1)}, u32[]{:S(2)}) copy-start(bf16[2,512,768]{2,1,0:T(8,128)(2,1)} %constant.2.clone.matrix_ref) | copy-start | bytes 4718596
  23.1 14.5 %all-to-all-start = ((bf16[32,16,128]{2,1,0:T(8,128)(2,1)}), bf16[32,16,128]{2,1,0:T(8,128)(2,1)S(1)}, u32[]{:S(2)}, u32[]{:S(2)}) async-start(bf16[32,16,128]{2,1,0:T(8,128)(2,1)} %get-tuple-element.25), calls=%async_computation | async-start | bytes 262144 | tf_op jit(solution)/shard_map/all_to_all | solution.py:414

commit v4 on v3

--- a/solution.py
+++ b/solution.py
@@ -16,7 +16,6 @@
 SINE_ROW = 40
 TABLE_ROWS = SINE_ROW + UV_MAX
 
-SMEM = pl.BlockSpec(memory_space=pltpu.SMEM)
 VMEM = pl.BlockSpec(memory_space=pltpu.VMEM)
 HBM = pl.BlockSpec(memory_space=pltpu.HBM)
 
@@ -50,27 +49,43 @@
 
 
 def table(coord):
-    row = lax.broadcasted_iota(jnp.int32, (TABLE_ROWS, coord.shape[1]), 0)
-    is_sine = row >= SINE_ROW
-    k = jnp.where(is_sine, row - (SINE_ROW - 1), row).astype(jnp.float32)
-    value = cos_turns(k * coord - jnp.where(is_sine, 0.25, 0.0))
-    return jnp.where((row > UV_MAX) & (row < SINE_ROW), 0.0, value)
-
-
-def tile_scratch(snap_tiles, blocks):
+    shape = (SUBLANES, coord.shape[1])
+    row = lax.broadcasted_iota(jnp.int32, shape, 0)
+    steps = UV_MAX // SUBLANES
+    fine = row.astype(jnp.float32) * coord
+    fine_cos, fine_sin = cos_turns(fine), cos_turns(fine - 0.25)
+    coarse_k = ((lax.rem(row, steps) + 1) * SUBLANES).astype(jnp.float32)
+    coarse = cos_turns(coarse_k * coord - jnp.where(row < steps, 0.0, 0.25))
+    cosines, sines = [fine_cos], [fine_sin]
+    for a in range(1, steps + 1):
+        step_cos, step_sin = coarse[a - 1 : a], coarse[steps + a - 1 : steps + a]
+        cosines.append(step_cos * fine_cos - step_sin * fine_sin)
+        sines.append(step_sin * fine_cos + step_cos * fine_sin)
+    cosines[-1] = jnp.where(row > 0, 0.0, cosines[-1])
+    sines[0] = jnp.where(row > 0, sines[0], sines.pop())
+    return jnp.concatenate([*cosines, *sines])
+
+
+def tile_scratch(tile_map, snap_tiles, blocks):
     local_snaps, chans, tiles, pix = snap_tiles.shape
     pitch = tiles + SUBLANES
     return [
+        pltpu.SMEM(tile_map.shape, jnp.int32),
+        pltpu.VMEM((local_snaps, tiles, pix), jnp.float32),
         pltpu.VMEM(snap_tiles.shape, jnp.bfloat16),
-        pltpu.SemaphoreType.DMA((local_snaps,)),
+        pltpu.SemaphoreType.DMA((local_snaps + 2,)),
         *[pltpu.VMEM((chans * pitch, pix), jnp.float32)] * 2,
         *[pltpu.VMEM((blocks * chans, pix), jnp.float32)] * 2,
     ]
 
 
-def tile_copies(tiles_ref, buffer, sems):
+def tile_copies(sources, map_ref, beam_ref, buffer, sems):
+    map_hbm, tiles_hbm, beam_hbm = sources
+    snaps = range(buffer.shape[0])
     return [
-        pltpu.make_async_copy(tiles_ref.at[s], buffer.at[s], sems.at[s]) for s in range(buffer.shape[0])
+        pltpu.make_async_copy(map_hbm, map_ref, sems.at[len(snaps)]),
+        pltpu.make_async_copy(beam_hbm, beam_ref, sems.at[len(snaps) + 1]),
+        *[pltpu.make_async_copy(tiles_hbm.at[s], buffer.at[s], sems.at[s]) for s in snaps],
     ]
 
 
@@ -78,9 +93,10 @@
     local_snaps, chans, tiles, pix = buffer.shape
     blocks = stage[0].shape[0] // chans
     pitch = tiles + SUBLANES
+    copies[0].wait()
+    copies[1].wait()
     for s in range(local_snaps):
-        if copies:
-            copies[s].wait()
+        copies[s + 2].wait()
         wide = spread[s % 2]
         for c in range(chans):
             wide[c * pitch : c * pitch + tiles, :] = buffer[s, c].astype(jnp.float32) * beam_ref[s]
@@ -99,9 +115,9 @@
     blocks = tile_map.shape[1] // snap_count
     count = (snap_count - 1) * PARTS
 
-    def body(map_ref, tiles_ref, beam_ref, *rest):
-        outs, (buffer, sems, *work) = rest[:count], rest[count:]
-        copies = tile_copies(tiles_ref, buffer, sems)
+    def body(map_hbm, tiles_hbm, beam_hbm, *rest):
+        outs, (map_ref, beam_ref, buffer, sems, *work) = rest[:count], rest[count:]
+        copies = tile_copies((map_hbm, tiles_hbm, beam_hbm), map_ref, beam_ref, buffer, sems)
         for copy in copies:
             copy.start()
         own = lax.axis_index("snap")
@@ -112,9 +128,9 @@
     return pl.pallas_call(
         body,
         out_shape=[pltpu.VMEM((blocks // PARTS * chans, local_snaps * pix), jnp.bfloat16)] * count,
-        in_specs=[SMEM, HBM, VMEM],
+        in_specs=[HBM, HBM, HBM],
         out_specs=[VMEM] * count,
-        scratch_shapes=tile_scratch(snap_tiles, blocks),
+        scratch_shapes=tile_scratch(tile_map, snap_tiles, blocks),
         compiler_params=limit(8),
         name="gather_tiles",
     )(tile_map, snap_tiles, beam_gain)
@@ -135,6 +151,20 @@
     return copies
 
 
+def fence(ref):
+    @pl.when(lax.axis_index("snap") < 0)
+    def _():
+        ref[...] = jnp.zeros(ref.shape, ref.dtype)
+
+
+def ahead_copy(kernel_ref, ahead_ref, sem, first_block, snap_count):
+    local_snaps, blocks = ahead_ref.shape[:2]
+    source = lax.rem(lax.axis_index("snap") + snap_count - 1, snap_count)
+    return pltpu.make_async_copy(
+        kernel_ref.at[pl.ds(source * local_snaps, local_snaps), pl.ds(first_block, blocks)], ahead_ref, sem
+    )
+
+
 def kernel_scratch(kernel, local_snaps, items):
     _, _, pix, width = kernel.shape
     slots = min(items, 4)
@@ -151,31 +181,38 @@
     return term[i * chans : (i + 1) * chans]
 
 
-def own_part(tile_map, snap_tiles, beam_gain, kernel, pixel_lm, columns, cells, snap_count):
+def own_part(tile_map, snap_tiles, beam_gain, kernel, pixel_lm, mode_uv, cells, snap_count):
     local_snaps, chans, tiles, pix = snap_tiles.shape
     blocks, width = kernel.shape[1], kernel.shape[3]
     groups = blocks // GROUP
     pixels = blocks * width
-
-    def body(map_ref, tiles_ref, beam_ref, kernel_ref, lm_ref, columns_ref, cube_ref, l_ref, m_ref, *rest):
-        ahead_ref, with_cos_ref, with_sin_ref, slots, kernel_sems, ahead_sem, gathered, buffer, sems, *work = rest
+    columns = 2 * mode_uv.shape[1]
+
+    def body(map_hbm, tiles_hbm, beam_hbm, kernel_ref, lm_hbm, uv_hbm, cube_ref, l_ref, m_ref, *rest):
+        ahead_ref, columns_ref, with_cos_ref, with_sin_ref, slots, kernel_sems, ahead_sem, gathered, *rest = rest
+        lm_ref, uv_ref, own_sems, *rest = rest
+        map_ref, beam_ref, buffer, sems, *work = rest
         own = lax.axis_index("snap")
-        copies = tile_copies(tiles_ref, buffer, sems)
-        for copy in copies:
+        copies = tile_copies((map_hbm, tiles_hbm, beam_hbm), map_ref, beam_ref, buffer, sems)
+        small = [
+            pltpu.make_async_copy(lm_hbm, lm_ref, own_sems.at[0]),
+            pltpu.make_async_copy(uv_hbm, uv_ref, own_sems.at[1]),
+        ]
+        for copy in [*small, *copies]:
             copy.start()
         weights = kernel_copies(kernel_ref, slots, kernel_sems, [own], local_snaps, range(groups))
         for copy in weights[: slots.shape[0]]:
             copy.start()
+        ahead = ahead_copy(kernel_ref, ahead_ref, ahead_sem, 0, snap_count)
+        ahead.start()
+        small[0].wait()
         m_ref[TABLE_ROWS:, :] = jnp.zeros((LANES - TABLE_ROWS, pixels), jnp.bfloat16)
         for b in range(blocks):
             part = slice(b * width, (b + 1) * width)
             l_ref[:, part] = table(lm_ref[0:1, part])
             m_ref[:TABLE_ROWS, part] = table(lm_ref[1:2, part]).astype(jnp.bfloat16)
-        source = lax.rem(own + snap_count - 1, snap_count)
-        ahead = pltpu.make_async_copy(
-            kernel_ref.at[pl.ds(source * local_snaps, local_snaps)], ahead_ref, ahead_sem
-        )
-        ahead.start()
+        small[1].wait()
+        pick_v(uv_ref, columns_ref, with_cos_ref, with_sin_ref, cells)
         collect(copies, own, [own], map_ref, buffer, beam_ref, work[:2], work[2:], [[gathered]])
         rows = GROUP * chans
         for g in range(groups):
@@ -187,7 +224,6 @@
                 cube_ref[start : start + chans, :] = group_term(group_tiles, slots.at[n], i, chans)
             if g + slots.shape[0] < groups:
                 weights[g + slots.shape[0]].start()
-        pick_v(columns_ref, with_cos_ref, with_sin_ref, cells)
         ahead.wait()
 
     return pl.pallas_call(
@@ -196,41 +232,50 @@
             pltpu.VMEM((blocks * chans, width), jnp.float32),
             pltpu.VMEM((TABLE_ROWS, pixels), jnp.float32),
             pltpu.VMEM((LANES, pixels), jnp.bfloat16),
-            pltpu.VMEM((local_snaps, blocks, pix, width), jnp.bfloat16),
-            pltpu.VMEM((LANES, columns.shape[1]), jnp.bfloat16),
-            pltpu.VMEM((LANES, columns.shape[1]), jnp.bfloat16),
+            pltpu.VMEM((local_snaps, GROUP, pix, width), jnp.bfloat16),
+            pltpu.VMEM((2, columns), jnp.int32),
+            pltpu.VMEM((LANES, columns), jnp.bfloat16),
+            pltpu.VMEM((LANES, columns), jnp.bfloat16),
         ),
-        in_specs=[SMEM, HBM, VMEM, HBM, VMEM, VMEM],
-        out_specs=(VMEM,) * 6,
+        in_specs=[HBM] * 6,
+        out_specs=(VMEM,) * 7,
         scratch_shapes=[
             *kernel_scratch(kernel, local_snaps, groups),
             pltpu.SemaphoreType.DMA,
             pltpu.VMEM((blocks * chans, local_snaps * pix), jnp.bfloat16),
-            *tile_scratch(snap_tiles, blocks),
+            pltpu.VMEM(pixel_lm.shape, jnp.float32),
+            pltpu.VMEM(mode_uv.shape, jnp.int32),
+            pltpu.SemaphoreType.DMA((2,)),
+            *tile_scratch(tile_map, snap_tiles, blocks),
         ],
         compiler_params=limit(24),
         name="own_part",
-    )(tile_map, snap_tiles, beam_gain, kernel, pixel_lm, columns)
-
-
-def pick_v(columns_ref, with_cos_ref, with_sin_ref, cells):
+    )(tile_map, snap_tiles, beam_gain, kernel, pixel_lm, mode_uv)
+
+
+def pick_v(uv_ref, columns_ref, with_cos_ref, with_sin_ref, cells):
     chunk = 2 * LANES
     lane = lax.broadcasted_iota(jnp.int32, (1, chunk), 1)
-    row = lax.broadcasted_iota(jnp.int32, (LANES, chunk), 0)
+    row = lax.broadcasted_iota(jnp.int32, (TABLE_ROWS, chunk), 0)
     for start in range(0, columns_ref.shape[1], chunk):
         part = slice(start, start + chunk)
         is_imag = lax.rem(lane, 2 * cells) >= cells
-        u, v = columns_ref[0:1, part], columns_ref[1:2, part]
+        modes = uv_ref[:, start // 2 : start // 2 + LANES]
+        owned = [modes[:, k : k + cells] for k in range(0, LANES, cells)]
+        both = jnp.concatenate([piece for piece in owned for _ in range(2)], axis=1)
+        columns_ref[:, part] = both
+        u, v = both[0:1], both[1:2]
         sign_u = jnp.where(u < 0, -1.0, 1.0)
         sign_v = jnp.where(v < 0, -1.0, 1.0)
         v = jnp.abs(v)
-        sin_row = jnp.where(v == 0, -1, v + (SINE_ROW - 1))
+        sin_row = jnp.where(v == 0, -1, SINE_ROW + lax.rem(v, UV_MAX))
         with_cos = jnp.where(row == jnp.where(is_imag, sin_row, v), jnp.where(is_imag, -sign_v, 1.0), 0.0)
         with_sin = jnp.where(
             row == jnp.where(is_imag, v, sin_row), jnp.where(is_imag, -sign_u, -sign_u * sign_v), 0.0
         )
-        with_cos_ref[:, part] = with_cos.astype(jnp.bfloat16)
-        with_sin_ref[:, part] = with_sin.astype(jnp.bfloat16)
+        empty = jnp.zeros((LANES - TABLE_ROWS, chunk), jnp.float32)
+        with_cos_ref[:, part] = jnp.concatenate([with_cos, empty]).astype(jnp.bfloat16)
+        with_sin_ref[:, part] = jnp.concatenate([with_sin, empty]).astype(jnp.bfloat16)
 
 
 def uv_part(others, kernel, ahead, partial, l_table, m_table, first_group, chans, begun=None, picks=None, cells=0):
@@ -260,8 +305,9 @@
             picked_sin = jnp.zeros((high, chunk), jnp.float32)
             for k in range(1, UV_MAX + 1):
                 hit = u == k
+                sin_at = k % UV_MAX * high
                 picked_cos = jnp.where(hit, at_cos[k * high : (k + 1) * high], picked_cos)
-                picked_sin = jnp.where(hit, at_sin[(k - 1) * high : k * high], picked_sin)
+                picked_sin = jnp.where(hit, at_sin[sin_at : sin_at + high], picked_sin)
             value = (picked_cos + picked_sin).astype(jnp.bfloat16)
             for k in range(0, chunk, 2 * cells):
                 out_ref[(start + k) // (2 * cells)] = value[:, k : k + 2 * cells]
@@ -272,7 +318,14 @@
         if last:
             begun_cube, begun_acc, columns_ref, with_cos_ref, with_sin_ref, sky_ref, out_ref, low, acc, lhs, *rest = rest
         else:
-            cube_ref, acc, low, *rest = rest
+            cube_ref, acc, next_ref, low, fetched, fetch_sems, *rest = rest
+            following = [
+                ahead_copy(kernel_ref, fetched, fetch_sems.at[0], GROUP, snap_count),
+                ahead_copy(kernel_ref, next_ref, fetch_sems.at[1], groups.stop * GROUP, snap_count),
+            ]
+            for copy in following:
+                copy.start()
+            fence(acc)
         if later:
             slots, sems = rest
             own = lax.axis_index("snap")
@@ -286,7 +339,12 @@
                 sky_ref[:, b, :] = begun_cube[b * chans : (b + 1) * chans, :]
         for n, g in enumerate(groups):
             sky = [partial_ref[g * rows + i * chans : g * rows + (i + 1) * chans, :] for i in range(GROUP)]
-            near = ahead_ref.at[:, g * GROUP : (g + 1) * GROUP]
+            near, at = ahead_ref, n * GROUP
+            if not last and n > 0:
+                near, at = fetched, at - GROUP
+                if n == 1:
+                    following[0].wait()
+            near = near.at[:, at : at + GROUP]
             group_tiles = tiles_refs[0][n * rows : (n + 1) * rows, :]
             sky = [sky[i] + group_term(group_tiles, near, i, chans) for i in range(GROUP)]
             for j in range(later):
@@ -327,6 +385,8 @@
             lhs[:, :LANES] = upper
             lhs[:, LANES:] = (total - upper.astype(jnp.float32)).astype(jnp.bfloat16)
             select(lhs, columns_ref, with_cos_ref, with_sin_ref, out_ref)
+        else:
+            following[1].wait()
 
     grid_shape = (cos_rows + sin_rows, LANES)
     scratch = [pltpu.VMEM((GROUP, high, width), jnp.float32)]
@@ -343,14 +403,17 @@
         out_shape = (
             pltpu.VMEM((groups.stop * rows, width), jnp.float32),
             pltpu.VMEM(grid_shape, jnp.float32),
+            pltpu.VMEM((local_snaps, blocks - groups.stop * GROUP, pix, width), jnp.bfloat16),
         )
+        fetched = (local_snaps, groups.stop * GROUP - GROUP, pix, width)
+        scratch += [pltpu.VMEM(fetched, jnp.bfloat16), pltpu.SemaphoreType.DMA((2,))]
     if later:
         scratch += kernel_scratch(kernel, local_snaps, len(groups) * later)
     return pl.pallas_call(
         body,
         out_shape=out_shape,
         in_specs=[HBM if operand is kernel else VMEM for operand in operands],
-        out_specs=(VMEM, VMEM),
+        out_specs=(VMEM,) * len(out_shape),
         scratch_shapes=scratch,
         compiler_params=limit(24 if later else 12),
         name="uv_last" if last else "uv_first",
@@ -395,22 +458,22 @@
     cells = mode_uv.shape[1] // owners
     pixel_total = pixel_lm.shape[1] * snap_count
 
-    snap_tiles, kernel, tile_map = (
-        pltpu.with_memory_space_constraint(value, pltpu.HBM) for value in (snap_tiles, kernel, tile_map)
+    snap_tiles, beam_gain, kernel, tile_map, pixel_lm, mode_uv = (
+        pltpu.with_memory_space_constraint(value, pltpu.HBM)
+        for value in (snap_tiles, beam_gain, kernel, tile_map, pixel_lm, mode_uv)
     )
-    sent = gather_tiles(tile_map, snap_tiles, pltpu.with_memory_space_constraint(beam_gain, pltpu.HBM), snap_count)
+    sent = gather_tiles(tile_map, snap_tiles, beam_gain, snap_count)
     others = [
         lax.ppermute(part, "snap", [(i, (i + n // PARTS + 1) % snap_count) for i in range(snap_count)])
         for n, part in enumerate(sent)
     ]
-    columns = jnp.broadcast_to(mode_uv.reshape(2, owners, 1, cells), (2, owners, 2, cells)).reshape(2, -1)
     partial, l_table, m_table, ahead, *picks = own_part(
-        tile_map, snap_tiles, beam_gain, kernel, pixel_lm, columns, cells, snap_count
+        tile_map, snap_tiles, beam_gain, kernel, pixel_lm, mode_uv, cells, snap_count
     )
-    shared = (kernel, ahead, partial, l_table, m_table)
-    begun = uv_part(others[0::PARTS], *shared, 0, chans)
+    shared = (partial, l_table, m_table)
+    *begun, ahead_next = uv_part(others[0::PARTS], kernel, ahead, *shared, 0, chans)
     half = kernel.shape[1] // GROUP // PARTS
-    sky, spread = uv_part(others[1::PARTS], *shared, half, chans, begun, (columns, *picks), cells)
+    sky, spread = uv_part(others[1::PARTS], kernel, ahead_next, *shared, half, chans, begun, picks, cells)
     regrouped = lax.all_to_all(spread, ("snap", "chan"), 0, 0, tiled=True)
     matrix = delay_matrix(length) / math.sqrt(pixel_total)
     matrix = matrix.transpose(1, 0, 2, 3).reshape(chan_count, chans, 4 * length)

time: 39 us -> 37.2 us (0.954)
  Pallas kernels: 20.1 us -> 18.5 us
    pallas_call x1, Pallas kernels: 7.35 us -> 6.26 us  [own_part(): pl.pallas_call(body, out_shape=(pltpu.VMEM((blocks * chans, width), jnp.f...]
    pallas_call x1, Pallas kernels: 2.62 us -> 1.68 us  [gather_tiles(): pl.pallas_call(body, out_shape=[pltpu.VMEM((blocks // PARTS * chans, loca...]
    pallas_call x2, Pallas kernels: 9.01 us -> 9.43 us  [uv_part(): pl.pallas_call(body, out_shape=out_shape, in_specs=[HBM if operand is ker...]
  transfers between devices with their start and end apart: 3 -> 3, of which waited for: 1 -> 1; matrix products, arithmetic and copies ran while one was open for 2% -> 2% of each run, Pallas kernels for 26% -> 25%
where the time goes in v4:
time: 37.2 us; the launch traced here: 36.9 us
  Pallas kernels  18.5 us (50%)
  starting transfers between devices  9.43 us (25%)
  waiting for transfers between devices  7.53 us (20%)
  local copies, waits for them, and re-layouts  0.69 us (2%)
  between operations  0.69 us (2%)
    pallas_call x2, Pallas kernels, uv_part(): pl.pallas_call(body, out_shape=out_shape, in_specs=[HBM if operand is ker...  9.43 us
    all_to_all x1, waiting for transfers between devices, per_device(): regrouped = lax.all_to_all(spread, ('snap', 'chan'), 0, 0, tiled=True)  7.52 us
    all_to_all x1, starting transfers between devices, per_device(): regrouped = lax.all_to_all(spread, ('snap', 'chan'), 0, 0, tiled=True)  6.29 us
    pallas_call x1, Pallas kernels, own_part(): pl.pallas_call(body, out_shape=(pltpu.VMEM((blocks * chans, width), jnp.f...  6.26 us
    ppermute x2, starting transfers between devices, per_device(): lax.ppermute(part, 'snap', [(i, (i + n // PARTS + 1) % snap_count) for i...  3.14 us
    pallas_call x1, Pallas kernels, gather_tiles(): pl.pallas_call(body, out_shape=[pltpu.VMEM((blocks // PARTS * chans, loca...  1.68 us
    pallas_call x1, Pallas kernels, delay_part(): pl.pallas_call(body, out_shape=jax.ShapeDtypeStruct((2, cells, length), j...  1.15 us
  transfers between devices with their start and end apart: 3, of which 1 were waited for; matrix products, arithmetic and copies ran while one was open for 2% of the time, Pallas kernels for 25%

profile of v4, /device:TPU:0, one launch (start us, length us, event | category | flops | bytes accessed | tf_op | source)
XLA Modules:
  0.0 36.9 jit_solution(4388784830899346794)
XLA Ops:
  0.6 1.7 %gather_tiles.1 = (bf16[96,1024]{1,0:T(8,128)(2,1)S(1)}, bf16[96,1024]{1,0:T(8,128)(2,1)S(1)}) custom-call(s32[16,32]{1,0:T(8,128)} %map_hbm.3, bf16[8,12,64,128]{3,2,1,0:T(8,128)(2,1)} %tiles_hbm.3, f32[8,64,128]{2,1,0:T(8,128)} %beam_hbm.3), custom_call_target="tpu_custom_call" | custom-call | tf_op jit(solution)/shard_map/gather_tiles/pallas_call | solution.py:128
  2.3 3.1 %collective-permute-start.1 = (bf16[96,1024]{1,0:T(8,128)(2,1)S(1)}, bf16[96,1024]{1,0:T(8,128)(2,1)S(1)}, u32[]{:S(2)}, u32[]{:S(2)}) collective-permute-start(bf16[96,1024]{1,0:T(8,128)(2,1)S(1)} %get-tuple-element.17), channel_id=1, source_target_pairs={{0,16},{16,0},{1,17},{17,1},{2,18},{18,2},{3,19},{19,3},{4,20},{20... | collective-permute-start | bytes 589832 | tf_op jit(solution)/shard_map/ppermute | solution.py:467
  5.4 0.1 collective-permute-start
  5.5 6.3 %own_part.1 = (f32[192,256]{1,0:T(8,128)S(1)}, f32[72,4096]{1,0:T(8,128)S(1)}, bf16[128,4096]{1,0:T(8,128)(2,1)S(1)}, bf16[8,4,128,256]{3,2,1,0:T(8,128)(2,1)S(1...) custom-call(s32[16,32]{1,0:T(8,128)} %map_hbm.3, ...), custom_call_target="tpu_custom_call" | custom-call | tf_op jit(solution)/shard_map/own_part/pallas_call | solution.py:229
  11.7 0.0 collective-permute-done.1.rest_0_
  11.7 3.1 %uv_first.1 = (f32[96,256]{1,0:T(8,128)S(1)}, f32[1040,128]{1,0:T(8,128)S(1)}, bf16[8,8,128,256]{3,2,1,0:T(8,128)(2,1)S(1)}) custom-call(bf16[96,1024]{1,0:T(8,128)(2,1)S(1)} %collective-permute-done.1.rest_0_, bf16[16,16,128,256]{3,2,1,0:T(8,128)(2,1)} %rest_1_.3, bf16[8,4,128,256]{3,2,1,0:T(8,128)(2,1)S(1)} %get-tuple-element.18.rest_2_, ...), custom_call_target="tpu_custom_call" | custom-call | tf_op jit(solution)/shard_map/uv_first/pallas_call | solution.py:412
  14.9 0.0 collective-permute-done.rest_0_
  14.9 0.0 copy-start
  14.9 6.3 %uv_last.1 = (f32[12,16,256]{2,1,0:T(8,128)S(1)}, bf16[32,16,128]{2,1,0:T(8,128)(2,1)}) custom-call(bf16[96,1024]{1,0:T(8,128)(2,1)S(1)} %collective-permute-done.rest_0_, bf16[16,16,128,256]{3,2,1,0:T(8,128)(2,1)} %rest_1_.3, bf16[8,8,128,256]{3,2,1,0:T(8,128)(2,1)S(1)} %get-tuple-element.22.rest_2_, f32[192,256]{1,0:T(8,128)S(1)} %get-tuple-element.19.rest_3_, ...), custom_call_target="tpu_custom_call" | custom-call | tf_op jit(solution)/shard_map/uv_last/pallas_call | solution.py:412
  21.2 6.3 %all-to-all-start = ((bf16[32,16,128]{2,1,0:T(8,128)(2,1)}), bf16[32,16,128]{2,1,0:T(8,128)(2,1)S(1)}, u32[]{:S(2)}, u32[]{:S(2)}) async-start(bf16[32,16,128]{2,1,0:T(8,128)(2,1)} %get-tuple-element.29), calls=%async_computation | async-start | bytes 262144 | tf_op jit(solution)/shard_map/all_to_all | solution.py:477
  27.5 0.7 %copy.9 = f32[16,12,256]{2,0,1:T(8,128)} copy(f32[16,12,256]{2,0,1:T(8,128)S(1)} %bitcast.3) | data formatting | bytes 393216
  28.2 7.5 %all-to-all-done = bf16[32,16,128]{2,1,0:T(8,128)(2,1)S(1)} async-done(((bf16[32,16,128]{2,1,0:T(8,128)(2,1)}), bf16[32,16,128]{2,1,0:T(8,128)(2,1)S(1)}, u32[]{:S(2)}, u32[]{:S(2)}) %all-to-all-start) | async-done | bytes 131104 | tf_op jit(solution)/shard_map/all_to_all | solution.py:477
  35.7 0.0 copy-done
  35.7 1.2 %delay_part.1 = f32[2,64,192]{2,1,0:T(8,128)} custom-call(bf16[512,128]{1,0:T(8,128)(2,1)S(1)} %bitcast.4, bf16[2,512,768]{2,1,0:T(8,128)(2,1)S(1)} %copy-done), custom_call_target="tpu_custom_call" | custom-call | tf_op jit(solution)/shard_map/delay_part/pallas_call | solution.py:441
Async XLA Ops:
  2.3 9.4 %collective-permute-start.1 = (bf16[96,1024]{1,0:T(8,128)(2,1)S(1)}, bf16[96,1024]{1,0:T(8,128)(2,1)S(1)}, u32[]{:S(2)}, u32[]{:S(2)}) collective-permute-start(bf16[96,1024]{1,0:T(8,128)(2,1)S(1)} %get-tuple-element.17), channel_id=1, source_target_pairs={{0,16},{16,0},{1,17},{17,1},{2,18},{18,2},{3,19},{19,3},{4,20},{20... | collective-permute-start | bytes 589832 | tf_op jit(solution)/shard_map/ppermute | solution.py:467
  5.4 9.5 %collective-permute-start = (bf16[96,1024]{1,0:T(8,128)(2,1)S(1)}, bf16[96,1024]{1,0:T(8,128)(2,1)S(1)}, u32[]{:S(2)}, u32[]{:S(2)}) collective-permute-start(bf16[96,1024]{1,0:T(8,128)(2,1)S(1)} %get-tuple-element.16), channel_id=1, source_target_pairs={{0,16},{16,0},{1,17},{17,1},{2,18},{18,2},{3,19},{19,3},{4,20},{20... | collective-permute-start | bytes 589832 | tf_op jit(solution)/shard_map/ppermute | solution.py:467
  14.9 20.8 %copy-start = (bf16[2,512,768]{2,1,0:T(8,128)(2,1)S(1)}, bf16[2,512,768]{2,1,0:T(8,128)(2,1)}, u32[]{:S(2)}) copy-start(bf16[2,512,768]{2,1,0:T(8,128)(2,1)} %constant.2.clone.matrix_ref) | copy-start | bytes 4718596
  21.2 14.5 %all-to-all-start = ((bf16[32,16,128]{2,1,0:T(8,128)(2,1)}), bf16[32,16,128]{2,1,0:T(8,128)(2,1)S(1)}, u32[]{:S(2)}, u32[]{:S(2)}) async-start(bf16[32,16,128]{2,1,0:T(8,128)(2,1)} %get-tuple-element.29), calls=%async_computation | async-start | bytes 262144 | tf_op jit(solution)/shard_map/all_to_all | solution.py:477

commit v5 on v4

--- a/solution.py
+++ b/solution.py
@@ -26,6 +26,10 @@
 
 def padded(chans):
     return -(-chans // SUBLANES) * SUBLANES
+
+
+def together(chans):
+    return SUBLANES // math.gcd(SUBLANES, chans)
 
 
 def delay_matrix(length):
@@ -66,37 +70,23 @@
     return jnp.concatenate([*cosines, *sines])
 
 
-def tile_scratch(tile_map, snap_tiles, blocks):
+def tile_scratch(tile_map, snap_tiles, blocks, copies):
     local_snaps, chans, tiles, pix = snap_tiles.shape
     pitch = tiles + SUBLANES
     return [
         pltpu.SMEM(tile_map.shape, jnp.int32),
-        pltpu.VMEM((local_snaps, tiles, pix), jnp.float32),
-        pltpu.VMEM(snap_tiles.shape, jnp.bfloat16),
-        pltpu.SemaphoreType.DMA((local_snaps + 2,)),
+        pltpu.SemaphoreType.DMA((copies,)),
         *[pltpu.VMEM((chans * pitch, pix), jnp.float32)] * 2,
         *[pltpu.VMEM((blocks * chans, pix), jnp.float32)] * 2,
     ]
 
 
-def tile_copies(sources, map_ref, beam_ref, buffer, sems):
-    map_hbm, tiles_hbm, beam_hbm = sources
-    snaps = range(buffer.shape[0])
-    return [
-        pltpu.make_async_copy(map_hbm, map_ref, sems.at[len(snaps)]),
-        pltpu.make_async_copy(beam_hbm, beam_ref, sems.at[len(snaps) + 1]),
-        *[pltpu.make_async_copy(tiles_hbm.at[s], buffer.at[s], sems.at[s]) for s in snaps],
-    ]
-
-
-def collect(copies, own, dests, map_ref, buffer, beam_ref, spread, stage, outs):
+def collect(ready, own, dests, map_ref, buffer, beam_ref, spread, stage, outs):
     local_snaps, chans, tiles, pix = buffer.shape
     blocks = stage[0].shape[0] // chans
     pitch = tiles + SUBLANES
-    copies[0].wait()
-    copies[1].wait()
     for s in range(local_snaps):
-        copies[s + 2].wait()
+        ready(s)
         wide = spread[s % 2]
         for c in range(chans):
             wide[c * pitch : c * pitch + tiles, :] = buffer[s, c].astype(jnp.float32) * beam_ref[s]
@@ -110,30 +100,51 @@
                 out[:, s * pix : (s + 1) * pix] = rows[i * size : (i + 1) * size, :].astype(jnp.bfloat16)
 
 
-def gather_tiles(tile_map, snap_tiles, beam_gain, snap_count):
+def gather_tiles(tile_map, snap_tiles, beam_gain, pixel_lm, mode_uv, snap_count):
     local_snaps, chans, tiles, pix = snap_tiles.shape
     blocks = tile_map.shape[1] // snap_count
     count = (snap_count - 1) * PARTS
-
-    def body(map_hbm, tiles_hbm, beam_hbm, *rest):
-        outs, (map_ref, beam_ref, buffer, sems, *work) = rest[:count], rest[count:]
-        copies = tile_copies((map_hbm, tiles_hbm, beam_hbm), map_ref, beam_ref, buffer, sems)
-        for copy in copies:
+    fetched = (snap_tiles, beam_gain, pixel_lm, mode_uv)
+
+    def body(map_hbm, tiles_hbm, beam_hbm, lm_hbm, uv_hbm, *rest):
+        outs, (buffer, beam_ref, lm_ref, uv_ref, map_ref, sems, *work) = rest[:count], rest[count:]
+        copies = [
+            pltpu.make_async_copy(source, target, sems.at[local_snaps + n])
+            for n, (source, target) in enumerate(
+                [(map_hbm, map_ref), (beam_hbm, beam_ref), (lm_hbm, lm_ref), (uv_hbm, uv_ref)]
+            )
+        ]
+        of_snap = [
+            pltpu.make_async_copy(tiles_hbm.at[s], buffer.at[s], sems.at[s]) for s in range(local_snaps)
+        ]
+        for copy in [*copies[:2], *of_snap, *copies[2:]]:
             copy.start()
         own = lax.axis_index("snap")
         dests = [lax.rem(own + j, snap_count) for j in range(1, snap_count)]
         outs = [outs[n : n + PARTS] for n in range(0, count, PARTS)]
-        collect(copies, own, dests, map_ref, buffer, beam_ref, work[:2], work[2:], outs)
+
+        def ready(s):
+            if s == 0:
+                copies[0].wait()
+                copies[1].wait()
+            of_snap[s].wait()
+
+        collect(ready, own, dests, map_ref, buffer, beam_ref, work[:2], work[2:], outs)
+        copies[2].wait()
+        copies[3].wait()
 
     return pl.pallas_call(
         body,
-        out_shape=[pltpu.VMEM((blocks // PARTS * chans, local_snaps * pix), jnp.bfloat16)] * count,
-        in_specs=[HBM, HBM, HBM],
-        out_specs=[VMEM] * count,
-        scratch_shapes=tile_scratch(tile_map, snap_tiles, blocks),
+        out_shape=[
+            *[pltpu.VMEM((blocks // PARTS * chans, local_snaps * pix), jnp.bfloat16)] * count,
+            *[pltpu.VMEM(value.shape, value.dtype) for value in fetched],
+        ],
+        in_specs=[HBM] * 5,
+        out_specs=[VMEM] * (count + len(fetched)),
+        scratch_shapes=tile_scratch(tile_map, snap_tiles, blocks, local_snaps + 4),
         compiler_params=limit(8),
         name="gather_tiles",
-    )(tile_map, snap_tiles, beam_gain)
+    )(tile_map, *fetched)
 
 
 def kernel_copies(kernel_ref, slots, sems, sources, local_snaps, groups):
@@ -188,32 +199,26 @@
     pixels = blocks * width
     columns = 2 * mode_uv.shape[1]
 
-    def body(map_hbm, tiles_hbm, beam_hbm, kernel_ref, lm_hbm, uv_hbm, cube_ref, l_ref, m_ref, *rest):
+    def body(map_hbm, buffer, beam_ref, kernel_ref, lm_ref, uv_ref, cube_ref, l_ref, m_ref, *rest):
         ahead_ref, columns_ref, with_cos_ref, with_sin_ref, slots, kernel_sems, ahead_sem, gathered, *rest = rest
-        lm_ref, uv_ref, own_sems, *rest = rest
-        map_ref, beam_ref, buffer, sems, *work = rest
+        map_ref, sems, *work = rest
         own = lax.axis_index("snap")
-        copies = tile_copies((map_hbm, tiles_hbm, beam_hbm), map_ref, beam_ref, buffer, sems)
-        small = [
-            pltpu.make_async_copy(lm_hbm, lm_ref, own_sems.at[0]),
-            pltpu.make_async_copy(uv_hbm, uv_ref, own_sems.at[1]),
-        ]
-        for copy in [*small, *copies]:
-            copy.start()
+        map_copy = pltpu.make_async_copy(map_hbm, map_ref, sems.at[0])
+        map_copy.start()
         weights = kernel_copies(kernel_ref, slots, kernel_sems, [own], local_snaps, range(groups))
         for copy in weights[: slots.shape[0]]:
             copy.start()
         ahead = ahead_copy(kernel_ref, ahead_ref, ahead_sem, 0, snap_count)
         ahead.start()
-        small[0].wait()
+        fence(cube_ref)
         m_ref[TABLE_ROWS:, :] = jnp.zeros((LANES - TABLE_ROWS, pixels), jnp.bfloat16)
         for b in range(blocks):
             part = slice(b * width, (b + 1) * width)
             l_ref[:, part] = table(lm_ref[0:1, part])
             m_ref[:TABLE_ROWS, part] = table(lm_ref[1:2, part]).astype(jnp.bfloat16)
-        small[1].wait()
         pick_v(uv_ref, columns_ref, with_cos_ref, with_sin_ref, cells)
-        collect(copies, own, [own], map_ref, buffer, beam_ref, work[:2], work[2:], [[gathered]])
+        map_copy.wait()
+        collect(lambda s: None, own, [own], map_ref, buffer, beam_ref, work[:2], work[2:], [[gathered]])
         rows = GROUP * chans
         for g in range(groups):
             n = g % slots.shape[0]
@@ -237,16 +242,13 @@
             pltpu.VMEM((LANES, columns), jnp.bfloat16),
             pltpu.VMEM((LANES, columns), jnp.bfloat16),
         ),
-        in_specs=[HBM] * 6,
+        in_specs=[HBM, VMEM, VMEM, HBM, VMEM, VMEM],
         out_specs=(VMEM,) * 7,
         scratch_shapes=[
             *kernel_scratch(kernel, local_snaps, groups),
             pltpu.SemaphoreType.DMA,
             pltpu.VMEM((blocks * chans, local_snaps * pix), jnp.bfloat16),
-            pltpu.VMEM(pixel_lm.shape, jnp.float32),
-            pltpu.VMEM(mode_uv.shape, jnp.int32),
-            pltpu.SemaphoreType.DMA((2,)),
-            *tile_scratch(tile_map, snap_tiles, blocks),
+            *tile_scratch(tile_map, snap_tiles, blocks, 1),
         ],
         compiler_params=limit(24),
         name="own_part",
@@ -284,31 +286,29 @@
     local_snaps = others[0].shape[1] // pix
     rows = GROUP * chans
     groups = range(first_group, first_group + others[0].shape[0] // rows)
-    high = padded(chans)
-    cos_rows, sin_rows = (UV_MAX + 1) * high, UV_MAX * high
+    high, q = padded(chans), together(chans)
+    span, tail = UV_MAX * chans, q * chans
+    grid_rows = 2 * span + tail
     later = len(others) - 1
     last = begun is not None
 
     def select(lhs, columns_ref, with_cos_ref, with_sin_ref, out_ref):
         chunk = 2 * LANES
+        which = lax.broadcasted_iota(jnp.int32, (tail, chunk), 0) // chans
         for start in range(0, columns_ref.shape[1], chunk):
             part = slice(start, start + chunk)
-            with_cos, with_sin = with_cos_ref[:, part], with_sin_ref[:, part]
-            at_cos = jnp.dot(
-                lhs[:cos_rows, :], jnp.concatenate([with_cos, with_cos]), preferred_element_type=jnp.float32
-            )
-            at_sin = jnp.dot(
-                lhs[cos_rows:, :], jnp.concatenate([with_sin, with_sin]), preferred_element_type=jnp.float32
-            )
-            u = jnp.broadcast_to(jnp.abs(columns_ref[0:1, part]), (high, chunk))
-            picked_cos = at_cos[:high]
-            picked_sin = jnp.zeros((high, chunk), jnp.float32)
-            for k in range(1, UV_MAX + 1):
-                hit = u == k
-                sin_at = k % UV_MAX * high
-                picked_cos = jnp.where(hit, at_cos[k * high : (k + 1) * high], picked_cos)
-                picked_sin = jnp.where(hit, at_sin[sin_at : sin_at + high], picked_sin)
-            value = (picked_cos + picked_sin).astype(jnp.bfloat16)
+            picks = jnp.concatenate([with_cos_ref[:, part], with_sin_ref[:, part]])
+            at_v = jnp.dot(lhs[...], picks, preferred_element_type=jnp.float32)
+            first_u = jnp.abs(columns_ref[0:1, part]) - which
+            picked = jnp.zeros((tail, chunk), jnp.float32)
+            for k in range(0, UV_MAX + 1, q):
+                picked = jnp.where(first_u == k, at_v[k * chans : k * chans + tail], picked)
+            value = picked[:chans]
+            for k in range(1, q):
+                value += picked[k * chans : (k + 1) * chans]
+            if high > chans:
+                value = jnp.concatenate([value, jnp.zeros((high - chans, chunk), jnp.float32)])
+            value = value.astype(jnp.bfloat16)
             for k in range(0, chunk, 2 * cells):
                 out_ref[(start + k) // (2 * cells)] = value[:, k : k + 2 * cells]
 
@@ -316,9 +316,9 @@
         tiles_refs, rest = rest[: len(others)], rest[len(others) :]
         kernel_ref, ahead_ref, partial_ref, l_ref, m_ref, *rest = rest
         if last:
-            begun_cube, begun_acc, columns_ref, with_cos_ref, with_sin_ref, sky_ref, out_ref, low, acc, lhs, *rest = rest
+            begun_cube, begun_acc, columns_ref, with_cos_ref, with_sin_ref, sky_ref, out_ref, acc, lhs, *rest = rest
         else:
-            cube_ref, acc, next_ref, low, fetched, fetch_sems, *rest = rest
+            cube_ref, acc, next_ref, fetched, fetch_sems, *rest = rest
             following = [
                 ahead_copy(kernel_ref, fetched, fetch_sems.at[0], GROUP, snap_count),
                 ahead_copy(kernel_ref, next_ref, fetch_sems.at[1], groups.stop * GROUP, snap_count),
@@ -333,7 +333,7 @@
             weights = kernel_copies(kernel_ref, slots, sems, sources, local_snaps, groups)
             for copy in weights[: slots.shape[0]]:
                 copy.start()
-        low[...] = jnp.zeros(low.shape, jnp.float32)
+        which = lax.broadcasted_iota(jnp.int32, (tail, width), 0) // chans
         if last:
             for b in range(first_group * GROUP):
                 sky_ref[:, b, :] = begun_cube[b * chans : (b + 1) * chans, :]
@@ -362,14 +362,15 @@
                     sky_ref[:, b, :] = sky[i]
                 else:
                     cube_ref[b * chans : (b + 1) * chans, :] = sky[i]
-                low[i, :chans, :] = sky[i].astype(jnp.bfloat16).astype(jnp.float32)
-                value = low[i][None]
-                waves = jnp.concatenate(
-                    [
-                        (l_ref[: UV_MAX + 1, part][:, None, :] * value).reshape(cos_rows, width),
-                        (l_ref[SINE_ROW:, part][:, None, :] * value).reshape(sin_rows, width),
-                    ]
-                ).astype(jnp.bfloat16)
+                low = sky[i].astype(jnp.bfloat16).astype(jnp.float32)
+                low = jnp.concatenate([low] * q)
+                waves = []
+                for r in [*range(0, UV_MAX, q), *range(SINE_ROW, TABLE_ROWS, q), UV_MAX]:
+                    wave = l_ref[r : r + 1, part]
+                    for k in range(1, q):
+                        wave = jnp.where(which < k, wave, l_ref[r + k : r + k + 1, part])
+                    waves.append(wave * low)
+                waves = jnp.concatenate(waves).astype(jnp.bfloat16)
                 term = lax.dot_general(
                     waves, m_ref[:, part], (((1,), (1,)), ((), ())), preferred_element_type=jnp.float32
                 )
@@ -380,16 +381,18 @@
                 else:
                     acc[...] = term
         if last:
-            total = acc[...]
-            upper = total.astype(jnp.bfloat16)
-            lhs[:, :LANES] = upper
-            lhs[:, LANES:] = (total - upper.astype(jnp.float32)).astype(jnp.bfloat16)
+            row = lax.broadcasted_iota(jnp.int32, (span, LANES), 0)
+            sines = acc[span : 2 * span, :]
+            lhs[:span, :LANES] = acc[:span, :].astype(jnp.bfloat16)
+            lhs[span:, :LANES] = acc[2 * span :, :].astype(jnp.bfloat16)
+            lhs[:span, LANES:] = jnp.where(row < chans, 0.0, sines).astype(jnp.bfloat16)
+            lhs[span:, LANES:] = jnp.where(row[:tail] < chans, sines[:tail], 0.0).astype(jnp.bfloat16)
             select(lhs, columns_ref, with_cos_ref, with_sin_ref, out_ref)
         else:
             following[1].wait()
 
-    grid_shape = (cos_rows + sin_rows, LANES)
-    scratch = [pltpu.VMEM((GROUP, high, width), jnp.float32)]
+    grid_shape = (grid_rows, LANES)
+    scratch = []
     operands = [*others, kernel, ahead, partial, l_table, m_table]
     if last:
         columns, with_cos, with_sin = picks
@@ -398,7 +401,7 @@
             pltpu.VMEM((chans, blocks, width), jnp.float32),
             pltpu.VMEM((columns.shape[1] // (2 * cells), high, 2 * cells), jnp.bfloat16),
         )
-        scratch += [pltpu.VMEM(grid_shape, jnp.float32), pltpu.VMEM((cos_rows + sin_rows, 2 * LANES), jnp.bfloat16)]
+        scratch += [pltpu.VMEM(grid_shape, jnp.float32), pltpu.VMEM((span + tail, 2 * LANES), jnp.bfloat16)]
     else:
         out_shape = (
             pltpu.VMEM((groups.stop * rows, width), jnp.float32),
@@ -462,7 +465,9 @@
         pltpu.with_memory_space_constraint(value, pltpu.HBM)
         for value in (snap_tiles, beam_gain, kernel, tile_map, pixel_lm, mode_uv)
     )
-    sent = gather_tiles(tile_map, snap_tiles, beam_gain, snap_count)
+    *sent, snap_tiles, beam_gain, pixel_lm, mode_uv = gather_tiles(
+        tile_map, snap_tiles, beam_gain, pixel_lm, mode_uv, snap_count
+    )
     others = [
         lax.ppermute(part, "snap", [(i, (i + n // PARTS + 1) % snap_count) for i in range(snap_count)])
         for n, part in enumerate(sent)

time: 37.2 us -> 34.6 us (0.930)
  Pallas kernels: 18.5 us -> 14.2 us
  waiting for transfers between devices: 7.53 us -> 9.58 us
    pallas_call x2, Pallas kernels: 9.43 us -> 7.17 us  [uv_part(): pl.pallas_call(body, out_shape=out_shape, in_specs=[HBM if operand is ker...]
    pallas_call x1, Pallas kernels: 6.26 us -> 4.11 us  [own_part(): pl.pallas_call(body, out_shape=(pltpu.VMEM((blocks * chans, width), jnp.f...]
    ppermute x2, waiting for transfers between devices: 0.01 us -> 2.06 us  [per_device(): lax.ppermute(part, 'snap', [(i, (i + n // PARTS + 1) % snap_count) for i...]
  transfers between devices with their start and end apart: 3 -> 3, of which waited for: 1 -> 3; matrix products, arithmetic and copies ran while one was open for 2% -> 2% of each run, Pallas kernels for 25% -> 20%
where the time goes in v5:
time: 34.6 us; the launch traced here: 34.3 us
  Pallas kernels  14.2 us (41%)
  waiting for transfers between devices  9.58 us (28%)
  starting transfers between devices  9.19 us (27%)
  local copies, waits for them, and re-layouts  0.68 us (2%)
  between operations  0.67 us (2%)
    all_to_all x1, waiting for transfers between devices, per_device(): regrouped = lax.all_to_all(spread, ('snap', 'chan'), 0, 0, tiled=True)  7.52 us
    pallas_call x2, Pallas kernels, uv_part(): pl.pallas_call(body, out_shape=out_shape, in_specs=[HBM if operand is ker...  7.17 us
    all_to_all x1, starting transfers between devices, per_device(): regrouped = lax.all_to_all(spread, ('snap', 'chan'), 0, 0, tiled=True)  6.06 us
    pallas_call x1, Pallas kernels, own_part(): pl.pallas_call(body, out_shape=(pltpu.VMEM((blocks * chans, width), jnp.f...  4.11 us
    ppermute x2, starting transfers between devices, per_device(): lax.ppermute(part, 'snap', [(i, (i + n // PARTS + 1) % snap_count) for i...  3.13 us
    ppermute x2, waiting for transfers between devices, per_device(): lax.ppermute(part, 'snap', [(i, (i + n // PARTS + 1) % snap_count) for i...  2.06 us
    pallas_call x1, Pallas kernels, gather_tiles(): pl.pallas_call(body, out_shape=[*[pltpu.VMEM((blocks // PARTS * chans, lo...  1.72 us
    pallas_call x1, Pallas kernels, delay_part(): pl.pallas_call(body, out_shape=jax.ShapeDtypeStruct((2, cells, length), j...  1.16 us
  transfers between devices with their start and end apart: 3, of which 3 were waited for; matrix products, arithmetic and copies ran while one was open for 2% of the time, Pallas kernels for 20%

profile of v5, /device:TPU:0, one launch (start us, length us, event | category | flops | bytes accessed | tf_op | source)
XLA Modules:
  0.0 34.3 jit_solution(88641804918685447)
XLA Ops:
  0.6 1.7 %gather_tiles.1 = (bf16[96,1024]{1,0:T(8,128)(2,1)S(1)}, bf16[96,1024]{1,0:T(8,128)(2,1)S(1)}, bf16[8,12,64,128]{3,2,1,0:T(8,128)(2,1)S(1)}, f32[8,64,128]{2,1,0...) custom-call(s32[16,32]{1,0:T(8,128)} %map_hbm.3, bf16[8,12,64,128]{3,2,1,0:T(8,128)(2,1)} %tiles_hbm.1, ...), custom_call_target="tpu_custom_call" | custom-call | tf_op jit(solution)/shard_map/gather_tiles/pallas_call | solution.py:136
  2.4 3.1 %collective-permute-start.1 = (bf16[96,1024]{1,0:T(8,128)(2,1)S(1)}, bf16[96,1024]{1,0:T(8,128)(2,1)S(1)}, u32[]{:S(2)}, u32[]{:S(2)}) collective-permute-start(bf16[96,1024]{1,0:T(8,128)(2,1)S(1)} %get-tuple-element.21), channel_id=1, source_target_pairs={{0,16},{16,0},{1,17},{17,1},{2,18},{18,2},{3,19},{19,3},{4,20},{20... | collective-permute-start | bytes 589832 | tf_op jit(solution)/shard_map/ppermute | solution.py:472
  5.4 0.1 collective-permute-start
  5.5 4.1 %own_part.1 = (f32[192,256]{1,0:T(8,128)S(1)}, f32[72,4096]{1,0:T(8,128)S(1)}, bf16[128,4096]{1,0:T(8,128)(2,1)S(1)}, bf16[8,4,128,256]{3,2,1,0:T(8,128)(2,1)S(1...) custom-call(s32[16,32]{1,0:T(8,128)} %map_hbm.3, ...), custom_call_target="tpu_custom_call" | custom-call | tf_op jit(solution)/shard_map/own_part/pallas_call | solution.py:234
  9.6 1.5 %collective-permute-done.1.rest_0_ = bf16[96,1024]{1,0:T(8,128)(2,1)S(1)} collective-permute-done((bf16[96,1024]{1,0:T(8,128)(2,1)S(1)}, bf16[96,1024]{1,0:T(8,128)(2,1)S(1)}, u32[]{:S(2)}, u32[]{:S(2)}) %collective-permute-start.1) | collective-permute-done | bytes 196640 | tf_op jit(solution)/shard_map/ppermute | solution.py:472
  11.2 2.8 %uv_first.1 = (f32[96,256]{1,0:T(8,128)S(1)}, f32[792,128]{1,0:T(8,128)S(1)}, bf16[8,8,128,256]{3,2,1,0:T(8,128)(2,1)S(1)}) custom-call(bf16[96,1024]{1,0:T(8,128)(2,1)S(1)} %collective-permute-done.1.rest_0_, bf16[16,16,128,256]{3,2,1,0:T(8,128)(2,1)} %rest_1_.3, bf16[8,4,128,256]{3,2,1,0:T(8,128)(2,1)S(1)} %get-tuple-element.26.rest_2_, ...), custom_call_target="tpu_custom_call" | custom-call | tf_op jit(solution)/shard_map/uv_first/pallas_call | solution.py:415
  14.0 0.5 %collective-permute-done.rest_0_ = bf16[96,1024]{1,0:T(8,128)(2,1)S(1)} collective-permute-done((bf16[96,1024]{1,0:T(8,128)(2,1)S(1)}, bf16[96,1024]{1,0:T(8,128)(2,1)S(1)}, u32[]{:S(2)}, u32[]{:S(2)}) %collective-permute-start) | collective-permute-done | bytes 196640 | tf_op jit(solution)/shard_map/ppermute | solution.py:472
  14.5 0.0 copy-start
  14.5 4.3 %uv_last.1 = (f32[12,16,256]{2,1,0:T(8,128)S(1)}, bf16[32,16,128]{2,1,0:T(8,128)(2,1)}) custom-call(bf16[96,1024]{1,0:T(8,128)(2,1)S(1)} %collective-permute-done.rest_0_, bf16[16,16,128,256]{3,2,1,0:T(8,128)(2,1)} %rest_1_.3, bf16[8,8,128,256]{3,2,1,0:T(8,128)(2,1)S(1)} %get-tuple-element.30.rest_2_, f32[192,256]{1,0:T(8,128)S(1)} %get-tuple-element.27.rest_3_, ...), custom_call_target="tpu_custom_call" | custom-call | tf_op jit(solution)/shard_map/uv_last/pallas_call | solution.py:415
  18.9 6.1 %all-to-all-start = ((bf16[32,16,128]{2,1,0:T(8,128)(2,1)}), bf16[32,16,128]{2,1,0:T(8,128)(2,1)S(1)}, u32[]{:S(2)}, u32[]{:S(2)}) async-start(bf16[32,16,128]{2,1,0:T(8,128)(2,1)} %get-tuple-element.37), calls=%async_computation | async-start | bytes 262144 | tf_op jit(solution)/shard_map/all_to_all | solution.py:482
  24.9 0.7 %copy.9 = f32[16,12,256]{2,0,1:T(8,128)} copy(f32[16,12,256]{2,0,1:T(8,128)S(1)} %bitcast.3) | data formatting | bytes 393216
  25.6 7.5 %all-to-all-done = bf16[32,16,128]{2,1,0:T(8,128)(2,1)S(1)} async-done(((bf16[32,16,128]{2,1,0:T(8,128)(2,1)}), bf16[32,16,128]{2,1,0:T(8,128)(2,1)S(1)}, u32[]{:S(2)}, u32[]{:S(2)}) %all-to-all-start) | async-done | bytes 131104 | tf_op jit(solution)/shard_map/all_to_all | solution.py:482
  33.1 0.0 copy-done
  33.1 1.2 %delay_part.1 = f32[2,64,192]{2,1,0:T(8,128)} custom-call(bf16[512,128]{1,0:T(8,128)(2,1)S(1)} %bitcast.4, bf16[2,512,768]{2,1,0:T(8,128)(2,1)S(1)} %copy-done), custom_call_target="tpu_custom_call" | custom-call | tf_op jit(solution)/shard_map/delay_part/pallas_call | solution.py:444
Async XLA Ops:
  2.4 8.8 %collective-permute-start.1 = (bf16[96,1024]{1,0:T(8,128)(2,1)S(1)}, bf16[96,1024]{1,0:T(8,128)(2,1)S(1)}, u32[]{:S(2)}, u32[]{:S(2)}) collective-permute-start(bf16[96,1024]{1,0:T(8,128)(2,1)S(1)} %get-tuple-element.21), channel_id=1, source_target_pairs={{0,16},{16,0},{1,17},{17,1},{2,18},{18,2},{3,19},{19,3},{4,20},{20... | collective-permute-start | bytes 589832 | tf_op jit(solution)/shard_map/ppermute | solution.py:472
  5.4 9.1 %collective-permute-start = (bf16[96,1024]{1,0:T(8,128)(2,1)S(1)}, bf16[96,1024]{1,0:T(8,128)(2,1)S(1)}, u32[]{:S(2)}, u32[]{:S(2)}) collective-permute-start(bf16[96,1024]{1,0:T(8,128)(2,1)S(1)} %get-tuple-element.20), channel_id=1, source_target_pairs={{0,16},{16,0},{1,17},{17,1},{2,18},{18,2},{3,19},{19,3},{4,20},{20... | collective-permute-start | bytes 589832 | tf_op jit(solution)/shard_map/ppermute | solution.py:472
  14.5 18.6 %copy-start = (bf16[2,512,768]{2,1,0:T(8,128)(2,1)S(1)}, bf16[2,512,768]{2,1,0:T(8,128)(2,1)}, u32[]{:S(2)}) copy-start(bf16[2,512,768]{2,1,0:T(8,128)(2,1)} %constant.2.clone.matrix_ref) | copy-start | bytes 4718596
  18.9 14.3 %all-to-all-start = ((bf16[32,16,128]{2,1,0:T(8,128)(2,1)}), bf16[32,16,128]{2,1,0:T(8,128)(2,1)S(1)}, u32[]{:S(2)}, u32[]{:S(2)}) async-start(bf16[32,16,128]{2,1,0:T(8,128)(2,1)} %get-tuple-element.37), calls=%async_computation | async-start | bytes 262144 | tf_op jit(solution)/shard_map/all_to_all | solution.py:482

commit v6 on v5

--- a/solution.py
+++ b/solution.py
@@ -76,7 +76,7 @@
     return [
         pltpu.SMEM(tile_map.shape, jnp.int32),
         pltpu.SemaphoreType.DMA((copies,)),
-        *[pltpu.VMEM((chans * pitch, pix), jnp.float32)] * 2,
+        *[pltpu.VMEM((padded(chans) * pitch, pix), jnp.float32)] * 2,
         *[pltpu.VMEM((blocks * chans, pix), jnp.float32)] * 2,
     ]
 

time: 34.6 us -> 34.6 us (level)
  no operation moved by 1% of the time
where the time goes in v6:
time: 34.6 us; the launch traced here: 34.3 us
  Pallas kernels  14.1 us (41%)
  waiting for transfers between devices  9.59 us (28%)
  starting transfers between devices  9.23 us (27%)
  local copies, waits for them, and re-layouts  0.68 us (2%)
  between operations  0.67 us (2%)
    all_to_all x1, waiting for transfers between devices, per_device(): regrouped = lax.all_to_all(spread, ('snap', 'chan'), 0, 0, tiled=True)  7.52 us
    pallas_call x2, Pallas kernels, uv_part(): pl.pallas_call(body, out_shape=out_shape, in_specs=[HBM if operand is ker...  7.16 us
    all_to_all x1, starting transfers between devices, per_device(): regrouped = lax.all_to_all(spread, ('snap', 'chan'), 0, 0, tiled=True)  6.08 us
    pallas_call x1, Pallas kernels, own_part(): pl.pallas_call(body, out_shape=(pltpu.VMEM((blocks * chans, width), jnp.f...  4.11 us
    ppermute x2, starting transfers between devices, per_device(): lax.ppermute(part, 'snap', [(i, (i + n // PARTS + 1) % snap_count) for i...  3.14 us
    ppermute x2, waiting for transfers between devices, per_device(): lax.ppermute(part, 'snap', [(i, (i + n // PARTS + 1) % snap_count) for i...  2.06 us
    pallas_call x1, Pallas kernels, gather_tiles(): pl.pallas_call(body, out_shape=[*[pltpu.VMEM((blocks // PARTS * chans, lo...  1.72 us
    pallas_call x1, Pallas kernels, delay_part(): pl.pallas_call(body, out_shape=jax.ShapeDtypeStruct((2, cells, length), j...  1.15 us
  transfers between devices with their start and end apart: 3, of which 3 were waited for; matrix products, arithmetic and copies ran while one was open for 2% of the time, Pallas kernels for 20%

profile of v6, /device:TPU:0, one launch (start us, length us, event | category | flops | bytes accessed | tf_op | source)
XLA Modules:
  0.0 34.3 jit_solution(15601307391379993310)
XLA Ops:
  0.6 1.7 %gather_tiles.1 = (bf16[96,1024]{1,0:T(8,128)(2,1)S(1)}, bf16[96,1024]{1,0:T(8,128)(2,1)S(1)}, bf16[8,12,64,128]{3,2,1,0:T(8,128)(2,1)S(1)}, f32[8,64,128]{2,1,0...) custom-call(s32[16,32]{1,0:T(8,128)} %map_hbm.3, bf16[8,12,64,128]{3,2,1,0:T(8,128)(2,1)} %tiles_hbm.1, ...), custom_call_target="tpu_custom_call" | custom-call | tf_op jit(solution)/shard_map/gather_tiles/pallas_call | solution.py:136
  2.4 3.1 %collective-permute-start.1 = (bf16[96,1024]{1,0:T(8,128)(2,1)S(1)}, bf16[96,1024]{1,0:T(8,128)(2,1)S(1)}, u32[]{:S(2)}, u32[]{:S(2)}) collective-permute-start(bf16[96,1024]{1,0:T(8,128)(2,1)S(1)} %get-tuple-element.21), channel_id=1, source_target_pairs={{0,16},{16,0},{1,17},{17,1},{2,18},{18,2},{3,19},{19,3},{4,20},{20... | collective-permute-start | bytes 589832 | tf_op jit(solution)/shard_map/ppermute | solution.py:472
  5.4 0.1 collective-permute-start
  5.5 4.1 %own_part.1 = (f32[192,256]{1,0:T(8,128)S(1)}, f32[72,4096]{1,0:T(8,128)S(1)}, bf16[128,4096]{1,0:T(8,128)(2,1)S(1)}, bf16[8,4,128,256]{3,2,1,0:T(8,128)(2,1)S(1...) custom-call(s32[16,32]{1,0:T(8,128)} %map_hbm.3, ...), custom_call_target="tpu_custom_call" | custom-call | tf_op jit(solution)/shard_map/own_part/pallas_call | solution.py:234
  9.6 1.5 %collective-permute-done.1.rest_0_ = bf16[96,1024]{1,0:T(8,128)(2,1)S(1)} collective-permute-done((bf16[96,1024]{1,0:T(8,128)(2,1)S(1)}, bf16[96,1024]{1,0:T(8,128)(2,1)S(1)}, u32[]{:S(2)}, u32[]{:S(2)}) %collective-permute-start.1) | collective-permute-done | bytes 196640 | tf_op jit(solution)/shard_map/ppermute | solution.py:472
  11.2 2.8 %uv_first.1 = (f32[96,256]{1,0:T(8,128)S(1)}, f32[792,128]{1,0:T(8,128)S(1)}, bf16[8,8,128,256]{3,2,1,0:T(8,128)(2,1)S(1)}) custom-call(bf16[96,1024]{1,0:T(8,128)(2,1)S(1)} %collective-permute-done.1.rest_0_, bf16[16,16,128,256]{3,2,1,0:T(8,128)(2,1)} %rest_1_.3, bf16[8,4,128,256]{3,2,1,0:T(8,128)(2,1)S(1)} %get-tuple-element.26.rest_2_, ...), custom_call_target="tpu_custom_call" | custom-call | tf_op jit(solution)/shard_map/uv_first/pallas_call | solution.py:415
  14.0 0.5 %collective-permute-done.rest_0_ = bf16[96,1024]{1,0:T(8,128)(2,1)S(1)} collective-permute-done((bf16[96,1024]{1,0:T(8,128)(2,1)S(1)}, bf16[96,1024]{1,0:T(8,128)(2,1)S(1)}, u32[]{:S(2)}, u32[]{:S(2)}) %collective-permute-start) | collective-permute-done | bytes 196640 | tf_op jit(solution)/shard_map/ppermute | solution.py:472
  14.5 0.0 copy-start
  14.5 4.3 %uv_last.1 = (f32[12,16,256]{2,1,0:T(8,128)S(1)}, bf16[32,16,128]{2,1,0:T(8,128)(2,1)}) custom-call(bf16[96,1024]{1,0:T(8,128)(2,1)S(1)} %collective-permute-done.rest_0_, bf16[16,16,128,256]{3,2,1,0:T(8,128)(2,1)} %rest_1_.3, bf16[8,8,128,256]{3,2,1,0:T(8,128)(2,1)S(1)} %get-tuple-element.30.rest_2_, f32[192,256]{1,0:T(8,128)S(1)} %get-tuple-element.27.rest_3_, ...), custom_call_target="tpu_custom_call" | custom-call | tf_op jit(solution)/shard_map/uv_last/pallas_call | solution.py:415
  18.9 6.1 %all-to-all-start = ((bf16[32,16,128]{2,1,0:T(8,128)(2,1)}), bf16[32,16,128]{2,1,0:T(8,128)(2,1)S(1)}, u32[]{:S(2)}, u32[]{:S(2)}) async-start(bf16[32,16,128]{2,1,0:T(8,128)(2,1)} %get-tuple-element.37), calls=%async_computation | async-start | bytes 262144 | tf_op jit(solution)/shard_map/all_to_all | solution.py:482
  24.9 0.7 %copy.9 = f32[16,12,256]{2,0,1:T(8,128)} copy(f32[16,12,256]{2,0,1:T(8,128)S(1)} %bitcast.3) | data formatting | bytes 393216
  25.6 7.5 %all-to-all-done = bf16[32,16,128]{2,1,0:T(8,128)(2,1)S(1)} async-done(((bf16[32,16,128]{2,1,0:T(8,128)(2,1)}), bf16[32,16,128]{2,1,0:T(8,128)(2,1)S(1)}, u32[]{:S(2)}, u32[]{:S(2)}) %all-to-all-start) | async-done | bytes 131104 | tf_op jit(solution)/shard_map/all_to_all | solution.py:482
  33.1 0.0 copy-done
  33.2 1.2 %delay_part.1 = f32[2,64,192]{2,1,0:T(8,128)} custom-call(bf16[512,128]{1,0:T(8,128)(2,1)S(1)} %bitcast.4, bf16[2,512,768]{2,1,0:T(8,128)(2,1)S(1)} %copy-done), custom_call_target="tpu_custom_call" | custom-call | tf_op jit(solution)/shard_map/delay_part/pallas_call | solution.py:444
Async XLA Ops:
  2.4 8.8 %collective-permute-start.1 = (bf16[96,1024]{1,0:T(8,128)(2,1)S(1)}, bf16[96,1024]{1,0:T(8,128)(2,1)S(1)}, u32[]{:S(2)}, u32[]{:S(2)}) collective-permute-start(bf16[96,1024]{1,0:T(8,128)(2,1)S(1)} %get-tuple-element.21), channel_id=1, source_target_pairs={{0,16},{16,0},{1,17},{17,1},{2,18},{18,2},{3,19},{19,3},{4,20},{20... | collective-permute-start | bytes 589832 | tf_op jit(solution)/shard_map/ppermute | solution.py:472
  5.4 9.1 %collective-permute-start = (bf16[96,1024]{1,0:T(8,128)(2,1)S(1)}, bf16[96,1024]{1,0:T(8,128)(2,1)S(1)}, u32[]{:S(2)}, u32[]{:S(2)}) collective-permute-start(bf16[96,1024]{1,0:T(8,128)(2,1)S(1)} %get-tuple-element.20), channel_id=1, source_target_pairs={{0,16},{16,0},{1,17},{17,1},{2,18},{18,2},{3,19},{19,3},{4,20},{20... | collective-permute-start | bytes 589832 | tf_op jit(solution)/shard_map/ppermute | solution.py:472
  14.5 18.6 %copy-start = (bf16[2,512,768]{2,1,0:T(8,128)(2,1)S(1)}, bf16[2,512,768]{2,1,0:T(8,128)(2,1)}, u32[]{:S(2)}) copy-start(bf16[2,512,768]{2,1,0:T(8,128)(2,1)} %constant.2.clone.matrix_ref) | copy-start | bytes 4718596
  18.9 14.3 %all-to-all-start = ((bf16[32,16,128]{2,1,0:T(8,128)(2,1)}), bf16[32,16,128]{2,1,0:T(8,128)(2,1)S(1)}, u32[]{:S(2)}, u32[]{:S(2)}) async-start(bf16[32,16,128]{2,1,0:T(8,128)(2,1)} %get-tuple-element.37), calls=%async_computation | async-start | bytes 262144 | tf_op jit(solution)/shard_map/all_to_all | solution.py:482
